TPU v7x, 512 devices: a whole 4x8x8 slice. The times are simulated.
512 devices in a mesh: lat: 64 (over y, z), lev: 8 (over x, core).
Axes of the slice: x: 4, y: 8, z: 8, core: 2. Of those that a mesh axis runs over, the one named last changes fastest.
Arguments:
- winds: float32 [2, 32, 2048, 1440], P(None, 'lev', 'lat'), may hold values from -6 to 6
- thickness: float32 [32, 2048, 1440], P('lev', 'lat'), may hold values from 0.5 to 2
- cutoff: int32 [2048], P('lat'), may hold values from 1 to 720, as said below
Outputs:
- new_winds: float32 [2, 32, 2048, 1440], P(None, 'lev', 'lat')
- new_thickness: float32 [32, 2048, 1440], P('lev', 'lat')
Inputs may be any that keep to these rules, and one draw needn't show every extreme that they name: Rows outside the 384 latitudes nearest each pole have a cutoff of half of 1440; rows inside have smaller cutoffs.
All inputs are finite; a program needn't handle non-finite values.
Results may differ from a plain program's by a relative error of at most 0.0003.
Values sent between devices are 32-bit elements; how exact they have to be, the bound alone decides.
A program may use at most 64 MiB of HBM per device.

v0:
```python
import math

import jax
import jax.numpy as jnp
from jax import lax
from jax.sharding import PartitionSpec as P

time_step = 0.2
coriolis = 1.0


def carried_in(value, axis, join, neutral):
    count, mine = (lax.axis_size(axis), lax.axis_index(axis))
    pieces = lax.all_gather(value, axis)
    pieces = pieces[::-1]
    mine = count - 1 - mine
    subtotal = jnp.full_like(value, 0) + jnp.asarray(neutral, value.dtype)

    def turn(position, subtotal):
        longer = join(subtotal, pieces[position])
        return jnp.where(position < mine, longer, subtotal)

    return lax.fori_loop(0, count - 1, turn, subtotal)


def extended(x, sides, width):
    for axis, dim in sides:
        count, length = (lax.axis_size(axis), x.shape[dim])
        up = [(i, (i + 1) % count) for i in range(count - 1)]
        down = [(j, i) for i, j in up]
        last = lax.slice_in_dim(x, length - width, length, axis=dim)
        leading = lax.slice_in_dim(x, 0, width, axis=dim)
        before = lax.ppermute(last, axis, up)
        after = lax.ppermute(leading, axis, down)
        x = jnp.concatenate([before, x, after], axis=dim)
    return x


def fourier_table(lon_count):
    column = jnp.arange(lon_count)
    middle = lon_count // 2
    wavenumber = jnp.where(column <= middle, column, column - middle)
    points = jnp.arange(lon_count)
    phase = points[:, None] * wavenumber[None, :] % lon_count
    angle = phase.astype(jnp.float32) * (2.0 * math.pi / lon_count)
    single = (wavenumber == 0) | (wavenumber == middle)
    weight = jnp.where(single, 1.0 / math.sqrt(lon_count), math.sqrt(2.0 / lon_count)).astype(
        jnp.float32
    )
    values = (
        jnp.where((column <= middle)[None, :], jnp.cos(angle), jnp.sin(angle)) * weight[None, :]
    )
    return (values, wavenumber.astype(jnp.float32))


def remove_high(vectors, cuts, fourier, wavenumber):
    coeffs = jnp.dot(vectors, fourier, precision=lax.Precision.HIGHEST)
    coeffs = jnp.where(wavenumber[None, :] > cuts[:, None], coeffs, 0.0)
    return vectors - jnp.dot(coeffs, fourier.T, precision=lax.Precision.HIGHEST)


def step_fields(zonal, merid, depth, geo_pad, depth_pad, merid_pad, first_row, lat_total):
    lat_rows = depth.shape[1]
    row_index = (first_row + jnp.arange(lat_rows)).astype(jnp.float32)
    center = (row_index + 0.5) * (math.pi / lat_total) - 0.5 * math.pi
    cos_center = jnp.cos(center)[None, :, None]
    sin_center = jnp.sin(center)[None, :, None]
    edge_index = (first_row + jnp.arange(lat_rows + 1)).astype(jnp.float32)
    edge = jnp.sin(edge_index * (math.pi / lat_total))[None, :, None]
    zonal_flux = (
        0.25 * (depth + jnp.roll(depth, -1, axis=2)) * (zonal + jnp.roll(zonal, -1, axis=2))
    )
    merid_flux = (
        0.25
        * (depth_pad[:, :-1] + depth_pad[:, 1:])
        * (merid_pad[:, :-1] + merid_pad[:, 1:])
        * edge
    )
    new_depth = depth - time_step * (
        zonal_flux - jnp.roll(zonal_flux, 1, axis=2) + (merid_flux[:, 1:] - merid_flux[:, :-1])
    )
    geo = geo_pad[:, 1:-1]
    new_zonal = zonal - time_step * (
        0.5 * (jnp.roll(geo, -1, axis=2) - jnp.roll(geo, 1, axis=2)) - coriolis * sin_center * merid
    )
    new_merid = merid - time_step * (
        0.5 * cos_center * (geo_pad[:, 2:] - geo_pad[:, :-2]) + coriolis * sin_center * zonal
    )
    return (new_zonal, new_merid, new_depth)


def add_terms(earlier, later):
    return earlier + later


def per_device(winds, thickness, cutoff):
    lat_count = lax.axis_size("lat")
    cap_devices = 3 * lat_count // 16
    position = lax.axis_index("lat")
    levels, lat_rows, lon_count = thickness.shape
    fourier, wavenumber = fourier_table(lon_count)
    fields = jnp.concatenate([winds, thickness[None]], axis=0)
    units = fields.reshape(-1, lon_count)
    unit_count = units.shape[0]
    unit_cut = jnp.broadcast_to(
        cutoff.astype(jnp.float32)[None, None, :], (3, levels, lat_rows)
    ).reshape(-1)
    is_polar = (position < cap_devices) | (position >= lat_count - cap_devices)
    per_peer = -(-unit_count // lat_count)
    padding = per_peer * lat_count - unit_count
    padded_units = jnp.concatenate([units, jnp.zeros((padding, lon_count), jnp.float32)], axis=0)
    padded_cut = jnp.concatenate(
        [unit_cut, jnp.full((padding,), float(lon_count // 2), jnp.float32)], axis=0
    )
    slot_data = lax.all_to_all(
        padded_units.reshape(lat_count, per_peer, lon_count),
        "lat",
        split_axis=0,
        concat_axis=0,
        tiled=True,
    )
    slot_cut = lax.all_to_all(
        padded_cut.reshape(lat_count, per_peer), "lat", split_axis=0, concat_axis=0, tiled=True
    )
    width = slot_data.shape[1]
    chosen = jnp.concatenate(
        [slot_data[:cap_devices], slot_data[lat_count - cap_devices :]], axis=0
    )
    chosen_cut = jnp.concatenate(
        [slot_cut[:cap_devices], slot_cut[lat_count - cap_devices :]], axis=0
    )
    cleaned = remove_high(
        chosen.reshape(-1, lon_count), chosen_cut.reshape(-1), fourier, wavenumber
    )
    cleaned = cleaned.reshape(2 * cap_devices, width, lon_count)
    middle = jnp.zeros((lat_count - 2 * cap_devices, width, lon_count), jnp.float32)
    outgoing = jnp.concatenate([cleaned[:cap_devices], middle, cleaned[cap_devices:]], axis=0)
    returned = lax.all_to_all(outgoing, "lat", split_axis=0, concat_axis=0, tiled=True)
    filtered_units = jnp.where(is_polar, returned.reshape(-1, lon_count), units)
    filtered = filtered_units.reshape(3, levels, lat_rows, lon_count)
    zonal, merid, depth = (filtered[0], filtered[1], filtered[2])
    local_below = jnp.cumsum(depth[::-1], axis=0)[::-1] - depth
    column = jnp.sum(depth, axis=0)
    from_below = carried_in(column, "lev", add_terms, jnp.zeros_like(column))
    geo = local_below + from_below[None] + 0.5 * depth
    stacked = jnp.stack([depth, merid, geo], axis=0)
    padded = extended(stacked, (("lat", 2),), 1)
    first_row = position * lat_rows
    new_zonal, new_merid, new_depth = step_fields(
        zonal, merid, depth, padded[2], padded[0], padded[1], first_row, lat_rows * lat_count
    )
    return (jnp.stack([new_zonal, new_merid], axis=0), new_depth)


def solution(mesh):
    return jax.shard_map(
        per_device,
        mesh=mesh,
        in_specs=(P(None, "lev", "lat", None), P("lev", "lat", None), P("lat")),
        out_specs=(P(None, "lev", "lat", None), P("lev", "lat", None)),
        check_vma=False,
    )
```

profile of v0, /device:TPU:1, one launch (start us, length us, event | category | flops | bytes accessed | tf_op | source)
XLA Modules:
  0.0 365.5 jit_solution(14404784713066660993)
XLA Ops:
  8.5 17.1 %all-to-all-start.1 = ((f32[64,1,6]{2,1,0:T(1,128)}), f32[64,1,6]{2,1,0:T(1,128)S(1)}, u32[]{:S(2)}, u32[]{:S(2)}) async-start(f32[64,1,6]{2,1,0:T(1,128)} %bitcast.1), calls=%async_computation.1 | async-start | bytes 65536 | tf_op jit(solution)/shard_map/all_to_all | solution.py:122
  25.7 1.9 pad_maximum_fusion.2
  27.6 1.9 reshape_reshape.4
  29.4 7.0 %all-to-all-done.1 = f32[64,1,6]{2,1,0:T(1,128)S(1)} async-done(((f32[64,1,6]{2,1,0:T(1,128)}), f32[64,1,6]{2,1,0:T(1,128)S(1)}, u32[]{:S(2)}, u32[]{:S(2)}) %all-to-all-start.1) | async-done | bytes 1568 | tf_op jit(solution)/shard_map/all_to_all | solution.py:122
  36.5 5.6 %all-to-all-start = ((f32[64,6,1440]{2,1,0:T(8,128)}), f32[64,6,1440]{2,1,0:T(8,128)}, u32[]{:S(2)}, u32[]{:S(2)}) async-start(f32[64,6,1440]{2,1,0:T(8,128)} %reshape_reshape.4), calls=%async_computation | async-start | bytes 6291456 | tf_op jit(solution)/shard_map/all_to_all | solution.py:115
  43.3 38.3 %select_multiply_fusion.11 = f32[1440,1440]{1,0:T(8,128)} fusion(f32[1440]{0:T(1024)S(1)} %or_select_fusion, s32[1440]{0:T(1024)S(1)} %get-tuple-element.125, pred[1440]{0:T(1024)(128)(4,1)S(1)} %iota_compare_fusion), kind=kLoop, calls=%fused_computation.4.clone.1.clone.clone.clone.1 | loop fusion | flops 22809600 | bytes 8307360 | tf_op jit(solution)/shard_map/dot_general | solution.py:57
  82.6 38.3 %all-to-all-done = f32[64,6,1440]{2,1,0:T(8,128)} async-done(((f32[64,6,1440]{2,1,0:T(8,128)}), f32[64,6,1440]{2,1,0:T(8,128)}, u32[]{:S(2)}, u32[]{:S(2)}) %all-to-all-start) | async-done | bytes 2211872 | tf_op jit(solution)/shard_map/all_to_all | solution.py:115
  121.0 1.3 fusion.46
  123.5 8.0 %fusion.20 = f32[144,1440]{1,0:T(8,128)S(1)} fusion(f32[144,1440]{1,0:T(8,128)} %reshape.155, f32[1440]{0:T(1024)} %get-tuple-element.126, f32[144]{0:T(256)} %gt.16, f32[1440,1440]{1,0:T(8,128)} %select_multiply_fusion.11), kind=kOutput, calls=%fused_computation.26 | convolution fusion | flops 3583595520 | bytes 9959616 | tf_op jit(solution)/shard_map/dot_general | solution.py:57
  131.5 46.4 %fusion.19 = f32[144,1440]{1,0:T(8,128)S(1)} fusion(f32[144,1440]{1,0:T(8,128)S(1)} %copy-done, f32[144,1440]{1,0:T(8,128)S(1)} %fusion.20, f32[1440]{0:T(1024)S(1)} %or_select_fusion, s32[1440]{0:T(1024)S(1)} %get-tuple-element.125, pred[1440]{0:T(1024)(128)(4,1)S(1)} %copy-done.3), kind=kOutput, calls=%fused_computation.25 | convolution fusion | flops 3606197760 | bytes 2501280 | tf_op jit(solution)/shard_map/dot_general | solution.py:59
  179.9 2.0 pad_maximum_fusion
  181.8 23.9 %all-to-all-start.2 = ((f32[64,6,1440]{2,1,0:T(8,128)}), f32[64,6,1440]{2,1,0:T(8,128)}, u32[]{:S(2)}, u32[]{:S(2)}) async-start(f32[64,6,1440]{2,1,0:T(8,128)} %pad_maximum_fusion), calls=%async_computation.2 | async-start | bytes 6291456 | tf_op jit(solution)/shard_map/all_to_all | solution.py:138
  205.8 75.5 %all-to-all-done.2 = f32[64,6,1440]{2,1,0:T(8,128)} async-done(((f32[64,6,1440]{2,1,0:T(8,128)}), f32[64,6,1440]{2,1,0:T(8,128)}, u32[]{:S(2)}, u32[]{:S(2)}) %all-to-all-start.2) | async-done | bytes 2211872 | tf_op jit(solution)/shard_map/all_to_all | solution.py:138
  281.3 3.6 reshape.156
  284.9 3.4 bitcast_select_fusion
  288.3 1.8 fusion.47
  294.2 38.7 %all-gather.3.cloned.1.call-done = f32[256,1440]{1,0:T(8,128)} async-done(((f32[32,1440]{1,0:T(8,128)}), f32[256,1440]{1,0:T(8,128)}) %all-gather.3.cloned.1.call-update) | async-done | bytes 1474576 | tf_op jit(solution)/shard_map/all_gather | solution.py:14
  332.9 2.7 rev.11
  335.5 7.1 %while.14 = (s32[]{:T(128)}, f32[32,1440]{1,0:T(8,128)S(1)}, s32[]{:T(128)}, f32[8,32,1440]{2,1,0:T(8,128)}, s32[]{:T(128)}, /*index=5*/s32[]{:T(128)}) while((s32[]{:T(128)}, f32[32,1440]{1,0:T(8,128)S(1)}, s32[]{:T(128)}, f32[8,32,1440]{2,1,0:T(8,128)}, s32[]{:T(128)}, /*index=5*/s32[]{:T(128)}) %tuple.49), condition=%wide.region_3.4_spmd.clone, body=%wide.region_2.3_spmd.clone.sunk | while | flops 138244 | bytes 553053 | solution.py:23
  342.7 2.0 fusion.37
  344.8 3.2 collective-permute-start
  348.0 1.3 collective-permute-start.1
  349.4 3.7 %collective-permute-done.1 = f32[3,4,1,1440]{3,2,1,0:T(1,128)S(1)} collective-permute-done((f32[3,4,1,1440]{3,2,1,0:T(1,128)S(1)}, f32[3,4,1,1440]{3,2,1,0:T(1,128)S(1)}, u32[]{:S(2)}, u32[]{:S(2)}) %collective-permute-start.1) | collective-permute-done | bytes 69152 | tf_op jit(solution)/shard_map/ppermute | solution.py:34
  356.4 2.3 fusion.26
  (59 shorter events, 21.3 us)
Async XLA Ops:
  8.5 27.9 %all-to-all-start.1 = ((f32[64,1,6]{2,1,0:T(1,128)}), f32[64,1,6]{2,1,0:T(1,128)S(1)}, u32[]{:S(2)}, u32[]{:S(2)}) async-start(f32[64,1,6]{2,1,0:T(1,128)} %bitcast.1), calls=%async_computation.1 | async-start | bytes 65536 | tf_op jit(solution)/shard_map/all_to_all | solution.py:122
  36.5 84.5 %all-to-all-start = ((f32[64,6,1440]{2,1,0:T(8,128)}), f32[64,6,1440]{2,1,0:T(8,128)}, u32[]{:S(2)}, u32[]{:S(2)}) async-start(f32[64,6,1440]{2,1,0:T(8,128)} %reshape_reshape.4), calls=%async_computation | async-start | bytes 6291456 | tf_op jit(solution)/shard_map/all_to_all | solution.py:115
  42.7 0.6 copy-start.2
  123.4 8.1 %copy-start = (f32[144,1440]{1,0:T(8,128)S(1)}, f32[144,1440]{1,0:T(8,128)}, u32[]{:S(2)}) copy-start(f32[144,1440]{1,0:T(8,128)} %reshape.155) | copy-start | bytes 2488324
  123.4 8.1 %copy-start.3 = (pred[1440]{0:T(1024)(128)(4,1)S(1)}, pred[1440]{0:T(1024)(128)(4,1)}, u32[]{:S(2)}) copy-start(pred[1440]{0:T(1024)(128)(4,1)} %copy-done.2) | copy-start | bytes 4324
  177.9 2.0 copy-start.4
  181.8 99.5 %all-to-all-start.2 = ((f32[64,6,1440]{2,1,0:T(8,128)}), f32[64,6,1440]{2,1,0:T(8,128)}, u32[]{:S(2)}, u32[]{:S(2)}) async-start(f32[64,6,1440]{2,1,0:T(8,128)} %pad_maximum_fusion), calls=%async_computation.2 | async-start | bytes 6291456 | tf_op jit(solution)/shard_map/all_to_all | solution.py:138
  205.8 127.1 %all-gather.3.cloned.1.call-start = ((), (), s32[]{:S(2)}) async-start(), calls=%async_computation.3 | async-start | bytes 1769472 | tf_op jit(solution)/shard_map/all_gather | solution.py:14
  294.2 48.5 %copy-start.1 = (f32[4,32,1439]{2,1,0:T(8,128)S(1)}, f32[4,32,1439]{2,1,0:T(8,128)}, u32[]{:S(2)}) copy-start(f32[4,32,1439]{2,1,0:T(8,128)} %slice.178) | copy-start | bytes 2210308
  344.8 4.6 %collective-permute-start = (f32[3,4,1,1440]{3,2,1,0:T(1,128)S(1)}, f32[3,4,1,1440]{3,2,1,0:T(1,128)S(1)}, u32[]{:S(2)}, u32[]{:S(2)}) collective-permute-start(f32[3,4,1,1440]{3,2,1,0:T(1,128)S(1)} %get-tuple-element.115), channel_id=1, source_target_pairs={{0,8},{8,16},{16,24},{24,32},{32,40},{40,48},{48,56},{56,64},{64,7... | collective-permute-start | bytes 207368 | tf_op jit(solution)/shard_map/ppermute | solution.py:33
  348.0 5.1 %collective-permute-start.1 = (f32[3,4,1,1440]{3,2,1,0:T(1,128)S(1)}, f32[3,4,1,1440]{3,2,1,0:T(1,128)S(1)}, u32[]{:S(2)}, u32[]{:S(2)}) collective-permute-start(f32[3,4,1,1440]{3,2,1,0:T(1,128)S(1)} %get-tuple-element.116), channel_id=1, source_target_pairs={{8,0},{16,8},{24,16},{32,24},{40,32},{48,40},{56,48},{64,56},{72,6... | collective-permute-start | bytes 207368 | tf_op jit(solution)/shard_map/ppermute | solution.py:34
Sparse Core Ops, SparseCore 0:
  290.9 41.9 all-gather.2
where the time goes:
time: 368 us; the launch traced here: 366 us
  waiting for transfers between devices  163 us (44%)
  other arithmetic  62.9 us (17%)
  matrix products  54.4 us (15%)
  starting transfers between devices  51.1 us (14%)
  local copies, waits for them, and re-layouts  19.5 us (5%)
  between operations  14.3 us (4%)
    all_to_all x1, waiting for transfers between devices, per_device(): lax.all_to_all(outgoing, 'lat', split_axis=0, concat_axis=0, tiled=True)  75.5 us
    dot_general x1, matrix products, remove_high(): return vectors - jnp.dot(coeffs, fourier.T, precision=lax.Precision.HIGHEST)  46.4 us
    all_gather x1, waiting for transfers between devices, carried_in(): pieces = lax.all_gather(value, axis)  38.7 us
    dot_general x1, other arithmetic, remove_high(): coeffs = jnp.dot(vectors, fourier, precision=lax.Precision.HIGHEST)  38.3 us
    all_to_all x1, waiting for transfers between devices, per_device(): lax.all_to_all(padded_units.reshape(lat_count, per_peer, lon_count), 'lat...  38.3 us
    all_to_all x1, starting transfers between devices, per_device(): lax.all_to_all(outgoing, 'lat', split_axis=0, concat_axis=0, tiled=True)  23.9 us
    all_to_all x1, starting transfers between devices, per_device(): lax.all_to_all(padded_cut.reshape(lat_count, per_peer), 'lat', split_axis...  17.1 us
    dot_general x1, matrix products, remove_high(): coeffs = jnp.dot(vectors, fourier, precision=lax.Precision.HIGHEST)  8.05 us
  transfers between devices with their start and end apart: 6, of which 5 were waited for; matrix products, arithmetic and copies ran while one was open for 13% of the time, Pallas kernels for 0%

commit v1 on v0

v1 whole, which is shorter than its diff:
```python
import functools
import math

import jax
import jax.numpy as jnp
import numpy as np
from jax import lax
from jax.experimental import pallas as pl
from jax.experimental.pallas import tpu as pltpu
from jax.sharding import PartitionSpec as P

MESH = pl.DeviceIdType.MESH
time_step = 0.2
coriolis = 1.0
RADIX = 12
HALO = 4
WIDE = 128
HALF3 = 0.5 * math.sqrt(3.0)


def filter_tables(lon):
    seg = lon // RADIX
    points = np.arange(WIDE) - HALO
    scale = math.sqrt(2.0 / lon)
    table = np.zeros((6, 2 * WIDE, 2 * WIDE))
    wave = np.full((6, 2 * WIDE), float(lon))
    turn = 2.0 * math.pi / lon
    j = np.arange(seg)
    for k in range(1, 6):
        m = RADIX * j + k
        angle = turn * ((points[:, None] * m[None, :]) % lon)
        table[k, :WIDE, :seg] = np.cos(angle) * scale
        table[k, :WIDE, WIDE : WIDE + seg] = np.sin(angle) * scale
        table[k, WIDE:, :seg] = -np.sin(angle) * scale
        table[k, WIDE:, WIDE : WIDE + seg] = np.cos(angle) * scale
        wave[k, :seg] = wave[k, WIDE : WIDE + seg] = np.minimum(m, lon - m)
    half = seg // 2
    m = RADIX * np.arange(half + 1)
    weight = np.where((m == 0) | (m == lon // 2), scale / math.sqrt(2.0), scale)
    angle = turn * ((points[:, None] * m[None, :]) % lon)
    table[0, :WIDE, : half + 1] = np.cos(angle) * weight
    table[0, :WIDE, half + 1 : seg] = np.sin(angle[:, 1:half]) * scale
    wave[0, : half + 1] = m
    wave[0, half + 1 : seg] = m[1:half]
    m = RADIX * np.arange(half) + RADIX // 2
    angle = turn * ((points[:, None] * m[None, :]) % lon)
    table[0, WIDE:, WIDE : WIDE + half] = np.cos(angle) * scale
    table[0, WIDE:, WIDE + half : WIDE + seg] = np.sin(angle) * scale
    wave[0, WIDE : WIDE + half] = wave[0, WIDE + half : WIDE + seg] = m
    table = table.astype(np.float32)
    high = table.astype(jnp.bfloat16)
    low = (table - high.astype(np.float32)).astype(jnp.bfloat16)
    return high, low, wave.astype(np.float32).reshape(1, 12 * WIDE)


def split(x):
    high = x.astype(jnp.bfloat16)
    return high, (x - high.astype(jnp.float32)).astype(jnp.bfloat16)


def forward12(x):
    e = [x[s] + x[s + 6] for s in range(6)]
    o = [x[s] - x[s + 6] for s in range(6)]
    ee = [e[s] + e[s + 3] for s in range(3)]
    eo = [e[s] - e[s + 3] for s in range(3)]
    sum12 = ee[1] + ee[2]
    d15, s15, d24, s24 = o[1] - o[5], o[1] + o[5], o[2] - o[4], o[2] + o[4]
    a, b = o[0] + 0.5 * d24, HALF3 * d15
    c, d = 0.5 * s15 + o[3], HALF3 * s24
    return [
        (ee[0] + sum12, eo[0] - eo[1] + eo[2]),
        (a + b, c + d),
        (eo[0] + 0.5 * (eo[1] - eo[2]), HALF3 * (eo[1] + eo[2])),
        (o[0] - d24, s15 - o[3]),
        (ee[0] - 0.5 * sum12, HALF3 * (ee[1] - ee[2])),
        (a - b, c - d),
    ]


def inverse12(z):
    (z0, z6), (r1, n1), (r2, n2), (r3, n3), (r4, n4), (r5, n5) = z
    a, b = HALF3 * (r1 - r5), 0.5 * (n1 + n5) + n3
    c, d = 0.5 * (r1 + r5) - r3, HALF3 * (n1 - n5)
    odd = [r1 + r3 + r5, b + a, c + d, n1 - n3 + n5, d - c, b - a]
    low, h4 = z0 - 0.5 * r4, HALF3 * n4
    ee = [z0 + r4, low + h4, low - h4]
    h2, hr = HALF3 * n2, 0.5 * r2
    eo = [z6 + r2, hr + h2 - z6, z6 - hr + h2]
    even = [ee[s] + eo[s] for s in range(3)] + [ee[s] - eo[s] for s in range(3)]
    return [even[s] + odd[s] for s in range(6)] + [even[s] - odd[s] for s in range(6)]


def lanes_of(shape):
    return lax.broadcasted_iota(jnp.int32, shape, len(shape) - 1)


def segments(tiles):
    lane = lanes_of(tiles[0].shape)
    out = [pltpu.roll(tiles[0], HALO, 1)]
    for s in range(1, RADIX):
        shift = 8 * s + HALO
        out.append(pltpu.roll(jnp.where(lane >= WIDE - shift, tiles[s - 1], tiles[s]), shift, 1))
    return out


def joined(segs):
    lane = lanes_of(segs[0].shape)
    out = []
    for t in range(RADIX):
        tile = pltpu.roll(segs[t], WIDE - (8 * t + HALO), 1)
        if t + 1 < RADIX:
            later = pltpu.roll(segs[t + 1], 116 - 8 * t, 1)
            tile = jnp.where(lane < 120 - 8 * t, tile, later)
        out.append(tile)
    return out


def forward_rows(tiles, y_high, y_low, row):
    lane = lanes_of((16, WIDE))
    inside = (lane >= HALO) & (lane < WIDE - HALO)
    classes = forward12(segments(tiles))
    for k, parts in enumerate(classes):
        for at, part in enumerate(parts):
            high, low = split(jnp.where(inside, part, 0.0))
            y_high[k, pl.ds(row, 16), at * WIDE : (at + 1) * WIDE] = high
            y_low[k, pl.ds(row, 16), at * WIDE : (at + 1) * WIDE] = low


def tiles_of(load):
    return [load(pl.ds(t * WIDE, WIDE)) for t in range(RADIX)]


def compute_kernel(
    lat_total,
    winds,
    thick,
    cutoff,
    below,
    edge_below,
    pack_minus,
    pack_plus,
    wave,
    f_high,
    f_low,
    new_winds,
    new_thick,
    y_high,
    y_low,
    z,
    field,
    result,
    cut,
):
    levels, rows = thick.shape[0], thick.shape[1]
    fields = 3 * levels
    main = fields * rows

    row8 = lax.broadcasted_iota(jnp.int32, (rows, WIDE), 0)
    column = jnp.zeros((rows, WIDE), jnp.float32)
    for r in range(rows):
        column = jnp.where(row8 == r, cutoff[r].astype(jnp.float32), column)
    for unit in range(fields + 1):
        cut[pl.ds(unit * rows, rows), :] = column
    at = main + rows
    minus_cut = pack_minus[:, pl.ds(1408, WIDE)][:, 64:65]
    plus_cut = pack_plus[:, pl.ds(1408, WIDE)][:, 64:65]
    cut[pl.ds(at, 8), :] = jnp.broadcast_to(minus_cut, (8, WIDE))
    cut[pl.ds(at + 8, 8), :] = jnp.broadcast_to(plus_cut, (8, WIDE))
    first = lax.broadcasted_iota(jnp.int32, (16, WIDE), 0) == 0
    cut[pl.ds(at + 16, 16), :] = jnp.where(first, minus_cut[0:1], plus_cut[0:1])

    def filter_unit(index, carry):
        base = index * rows
        for half in range(rows // 16):
            @pl.when(index < 2 * levels)
            def _():
                side, level = index // levels, index % levels
                forward_rows(tiles_of(lambda c: winds[side, level, pl.ds(half * 16, 16), c]), y_high, y_low, base + half * 16)
            @pl.when((index >= 2 * levels) & (index < fields))
            def _():
                forward_rows(tiles_of(lambda c: thick[index - 2 * levels, pl.ds(half * 16, 16), c]), y_high, y_low, base + half * 16)
        return carry

    lax.fori_loop(0, fields, filter_unit, 0)
    for half in range(rows // 16):
        forward_rows(tiles_of(lambda c: below[pl.ds(half * 16, 16), c]), y_high, y_low, main + half * 16)
    forward_rows(tiles_of(lambda c: jnp.concatenate([pack_minus[:, c], pack_plus[:, c]], axis=0)), y_high, y_low, at)
    forward_rows(tiles_of(lambda c: jnp.concatenate([edge_below[:, c], jnp.zeros((8, WIDE), jnp.float32)], axis=0)), y_high, y_low, at + 16)

    for k in range(6):
        high, low = f_high[k], f_low[k]
        yh, yl = y_high[k], y_low[k]
        coeffs = jnp.dot(
            jnp.concatenate([yh, yl, yh], axis=1),
            jnp.concatenate([high, high, low], axis=0),
            preferred_element_type=jnp.float32,
        )
        limit = cut[...]
        wanted = wave[:, pl.ds(k * 2 * WIDE, 2 * WIDE)]
        keep = jnp.concatenate([limit >= wanted[:, :WIDE], limit >= wanted[:, WIDE:]], axis=1)
        xh, xl = split(jnp.where(keep, coeffs, 0.0))
        z[k] = lax.dot_general(
            jnp.concatenate([xh, xl, xh], axis=1),
            jnp.concatenate([high, high, low], axis=1),
            (((1,), (1,)), ((), ())),
            preferred_element_type=jnp.float32,
        )

    def back(index, carry):
        for half in range(rows // 16):
            here = pl.ds(index * rows + half * 16, 16)
            parts = [(z[k, here, :WIDE], z[k, here, WIDE:]) for k in range(6)]
            for s, value in enumerate(inverse12(parts)):
                field[index, s, pl.ds(half * 16, 16), :] = value
        return carry

    lax.fori_loop(0, fields + 2, back, 0)

    lat = lax.axis_index("lat")
    row_index = (lat * rows + row8).astype(jnp.float32)
    center = (row_index + 0.5) * (math.pi / lat_total) - 0.5 * math.pi
    sin_center = (time_step * coriolis) * jnp.sin(center)
    cos_center = (0.5 * time_step) * jnp.cos(center)
    edge = (0.25 * time_step) * jnp.sin(row_index * (math.pi / lat_total))
    last_index = (lat * rows + rows + jnp.zeros((1, WIDE), jnp.int32)).astype(jnp.float32)
    last_edge = (0.25 * time_step) * jnp.sin(last_index * (math.pi / lat_total))
    top, bottom = row8 == 0, row8 == rows - 1

    def down(x, halo):
        return jnp.where(top, halo, pltpu.roll(x, 1, 0))

    def up(x, halo):
        return jnp.where(bottom, halo, pltpu.roll(x, rows - 1, 0))

    def east(x):
        return pltpu.roll(x, WIDE - 1, 1)

    def west(x):
        return pltpu.roll(x, 1, 1)

    def stencil(s, carry):
        total = field[fields, s]
        outside = field[fields + 1, s]
        minus_total, plus_total = outside[16:17], outside[17:18]
        for level in reversed(range(levels)):
            u, v, h = field[level, s], field[levels + level, s], field[2 * levels + level, s]
            hm, vm = outside[level : level + 1], outside[levels + level : levels + level + 1]
            hp, vp = outside[8 + level : 9 + level], outside[8 + levels + level : 9 + levels + level]
            geo = total + 0.5 * h
            geo_minus, geo_plus = minus_total + 0.5 * hm, plus_total + 0.5 * hp
            total, minus_total, plus_total = total + h, minus_total + hm, plus_total + hp
            zonal = (0.25 * time_step) * (h + east(h)) * (u + east(u))
            merid = (h + down(h, hm)) * (v + down(v, vm)) * edge
            beyond = (h[rows - 1 :] + hp) * (v[rows - 1 :] + vp) * last_edge
            result[2 * levels + level, s] = h - ((zonal - west(zonal)) + (up(merid, beyond) - merid))
            result[level, s] = u - (0.5 * time_step) * (east(geo) - west(geo)) + sin_center * v
            result[levels + level, s] = v - cos_center * (up(geo, geo_plus) - down(geo, geo_minus)) - sin_center * u
        return carry

    lax.fori_loop(0, RADIX, stencil, 0)

    def write(index, carry):
        for part in range(rows // 8):
            here = pl.ds(part * 8, 8)
            tiles = joined([result[index, s, here, :] for s in range(RADIX)])
            @pl.when(index < 2 * levels)
            def _():
                for t in range(RADIX):
                    new_winds[index // levels, index % levels, here, t * WIDE : (t + 1) * WIDE] = tiles[t]
            @pl.when(index >= 2 * levels)
            def _():
                for t in range(RADIX):
                    new_thick[index - 2 * levels, here, t * WIDE : (t + 1) * WIDE] = tiles[t]
        return carry

    lax.fori_loop(0, fields, write, 0)


def compute(lat_total, winds, thick, cutoff, below, edge_below, pack_minus, pack_plus):
    levels, rows, lon = thick.shape
    high, low, wave = filter_tables(lon)
    full = RADIX * WIDE
    units = (3 * levels + 2) * rows
    whole = lambda shape: pl.BlockSpec(shape, lambda i: (0,) * len(shape), pipeline_mode=pl.Buffered(1))
    return pl.pallas_call(
        functools.partial(compute_kernel, lat_total),
        grid=(1,),
        out_shape=(
            jax.ShapeDtypeStruct(winds.shape, jnp.float32),
            jax.ShapeDtypeStruct(thick.shape, jnp.float32),
        ),
        in_specs=[
            whole((2, levels, rows, full)),
            whole((levels, rows, full)),
            pl.BlockSpec(memory_space=pltpu.SMEM),
            whole((rows, full)),
            whole((8, full)),
            whole((8, full)),
            whole((8, full)),
            whole((1, full)),
            whole(high.shape),
            whole(low.shape),
        ],
        out_specs=(whole((2, levels, rows, full)), whole((levels, rows, full))),
        scratch_shapes=[
            pltpu.VMEM((6, units, 2 * WIDE), jnp.bfloat16),
            pltpu.VMEM((6, units, 2 * WIDE), jnp.bfloat16),
            pltpu.VMEM((6, units, 2 * WIDE), jnp.float32),
            pltpu.VMEM((3 * levels + 2, RADIX, rows, WIDE), jnp.float32),
            pltpu.VMEM((3 * levels, RADIX, rows, WIDE), jnp.float32),
            pltpu.VMEM((units, WIDE), jnp.float32),
        ],
        compiler_params=pltpu.CompilerParams(vmem_limit_bytes=56 << 20),
    )(winds, thick, cutoff, below, edge_below, pack_minus, pack_plus, jnp.asarray(wave), jnp.asarray(high), jnp.asarray(low))


def exchange_kernel(
    lat_count,
    lev_count,
    thick,
    winds,
    cutoff,
    below,
    edge_below,
    out_minus,
    out_plus,
    merid,
    send_minus,
    send_plus,
    from_minus,
    from_plus,
    column,
    pair,
    sums,
    chained,
    shared,
    row_column,
    row_pair,
    row_sums,
    row_chained,
    row_shared,
    local_sem,
    send_sem,
    recv_sem,
):
    levels, rows, lon = thick.shape
    full = RADIX * WIDE
    part = rows // 2
    lat, lev = lax.axis_index("lat"), lax.axis_index("lev")
    x, core = lev // 2, lev % 2
    chips = lev_count // 2
    lat_up, lat_down = (lat + 1) % lat_count, (lat + lat_count - 1) % lat_count
    partner = x * 2 + (1 - core)
    x_up, x_down = ((x + 1) % chips) * 2 + core, ((x + chips - 1) % chips) * 2 + core

    barrier = pltpu.get_barrier_semaphore()
    around = [(lat_up, lev), (lat_down, lev), (lat, partner), (lat, x_up), (lat, x_down)]
    for device in around:
        pl.semaphore_signal(barrier, inc=1, device_id=device, device_id_type=MESH)

    loads = [
        pltpu.make_async_copy(winds.at[1, :, pl.ds(at, 8), :], merid.at[i], local_sem.at[i])
        for i, at in enumerate((0, rows - 8))
    ]
    for load in loads:
        load.start()

    def remote(source, target, at, device):
        return pltpu.make_async_remote_copy(
            src_ref=source,
            dst_ref=target,
            send_sem=send_sem.at[at],
            recv_sem=recv_sem.at[at],
            device_id=device,
            device_id_type=MESH,
        )

    total = thick[0]
    for level in range(1, levels):
        total = total + thick[level]
    column[:, pl.ds(full - WIDE, WIDE)] = jnp.zeros((rows, WIDE), jnp.float32)
    column[:, pl.ds(0, lon)] = total
    for load in loads:
        load.wait()
    lane8 = lanes_of((8, WIDE))
    row8 = lax.broadcasted_iota(jnp.int32, (8, lon), 0)
    for which, (pack, row) in enumerate(((send_minus, 0), (send_plus, rows - 1))):
        inner = row % 8
        value = jnp.zeros((8, lon), jnp.float32)
        for level in range(levels):
            value = jnp.where(row8 == level, thick[level, row : row + 1, :], value)
            value = jnp.where(row8 == levels + level, merid[which, level, inner : inner + 1, :], value)
        limit = cutoff[row].astype(jnp.float32)
        pack[:, pl.ds(full - WIDE, WIDE)] = jnp.broadcast_to(limit, (8, WIDE))
        pack[:, pl.ds(0, lon)] = value

    pl.semaphore_wait(barrier, len(around))
    mine, theirs = pl.multiple_of(core * part, part), pl.multiple_of((1 - core) * part, part)
    to_minus = remote(send_minus, from_plus, 0, (lat_down, lev))
    to_plus = remote(send_plus, from_minus, 1, (lat_up, lev))
    to_pair = remote(column.at[pl.ds(theirs, part), :], pair, 2, (lat, partner))
    to_pair.start()
    to_minus.start()
    to_plus.start()

    to_pair.wait()
    own = column[pl.ds(mine, part), :]
    sums[...] = own + pair[...]
    links = [remote(sums.at[pl.ds(8 * i, 8), :], chained.at[pl.ds(8 * i, 8), :], 3 + i, (lat, x_down)) for i in range(2)]
    row_link = remote(row_sums, row_chained, 5, (lat, x_down))

    @pl.when(x == chips - 1)
    def _():
        chained[...] = jnp.zeros_like(chained)
        row_chained[...] = jnp.zeros_like(row_chained)
        for link in links:
            link.start()

    to_minus.wait()
    to_plus.wait()
    keep_minus = jnp.where(lat == 0, 0.0, 1.0)
    keep_plus = jnp.where(lat == lat_count - 1, 0.0, 1.0)
    value_minus, value_plus = from_minus[...] * keep_minus, from_plus[...] * keep_plus
    out_minus[...] = value_minus
    out_plus[...] = value_plus
    sum_minus, sum_plus = value_minus[0:1], value_plus[0:1]
    for level in range(1, levels):
        sum_minus = sum_minus + value_minus[level : level + 1]
        sum_plus = sum_plus + value_plus[level : level + 1]
    row_column[0] = jnp.where(core == 0, sum_minus, sum_plus)
    row_column[1] = jnp.where(core == 0, sum_plus, sum_minus)
    to_row_pair = remote(row_column.at[1], row_pair, 6, (lat, partner))
    to_row_pair.start()

    for i, link in enumerate(links):
        @pl.when(x < chips - 1)
        def _():
            link.wait_recv()
        @pl.when((x < chips - 1) & (x > 0))
        def _():
            sums[pl.ds(8 * i, 8), :] = sums[pl.ds(8 * i, 8), :] + chained[pl.ds(8 * i, 8), :]
            link.start()

    to_row_pair.wait()
    row_sums[...] = row_column[0] + row_pair[...]

    @pl.when(x == chips - 1)
    def _():
        row_link.start()

    upper = jnp.where(core == 0, 0.0, 1.0)
    column[pl.ds(mine, part), :] = chained[...] + upper * own
    share = remote(column.at[pl.ds(mine, part), :], shared, 7, (lat, partner))
    share.start()

    @pl.when(x < chips - 1)
    def _():
        row_link.wait_recv()

    @pl.when((x < chips - 1) & (x > 0))
    def _():
        row_sums[...] = row_sums[...] + row_chained[...]
        row_link.start()

    row_column[0] = row_chained[...] + upper * row_column[0]
    row_share = remote(row_column.at[0], row_shared, 8, (lat, partner))
    row_share.start()

    lower = 1.0 - upper
    share.wait_recv()
    below[pl.ds(mine, part), :] = (chained[...] + lower * pair[...])[:, :lon]
    below[pl.ds(theirs, part), :] = shared[...][:, :lon]
    row_share.wait_recv()
    first = (row_chained[...] + lower * row_pair[...])[:, :lon]
    second = row_shared[...][:, :lon]
    edge_below[...] = jnp.zeros_like(edge_below)
    edge_below[0:1, :] = jnp.where(core == 0, first, second)
    edge_below[1:2, :] = jnp.where(core == 0, second, first)

    share.wait_send()
    row_share.wait_send()

    @pl.when(x > 0)
    def _():
        for link in links:
            link.wait_send()
        row_link.wait_send()


def exchange(mesh_shape, winds, thick, cutoff):
    levels, rows, lon = thick.shape
    full = RADIX * WIDE
    part = rows // 2
    vmem = pl.BlockSpec(memory_space=pltpu.VMEM)
    return pl.pallas_call(
        functools.partial(exchange_kernel, mesh_shape["lat"], mesh_shape["lev"]),
        out_shape=(
            jax.ShapeDtypeStruct((rows, lon), jnp.float32),
            jax.ShapeDtypeStruct((8, lon), jnp.float32),
            jax.ShapeDtypeStruct((8, full), jnp.float32),
            jax.ShapeDtypeStruct((8, full), jnp.float32),
        ),
        in_specs=[vmem, pl.BlockSpec(memory_space=pl.ANY), pl.BlockSpec(memory_space=pltpu.SMEM)],
        out_specs=(vmem, vmem, vmem, vmem),
        scratch_shapes=[
            pltpu.VMEM((2, levels, 8, lon), jnp.float32),
            pltpu.VMEM((8, full), jnp.float32),
            pltpu.VMEM((8, full), jnp.float32),
            pltpu.VMEM((8, full), jnp.float32),
            pltpu.VMEM((8, full), jnp.float32),
            pltpu.VMEM((rows, full), jnp.float32),
            pltpu.VMEM((part, full), jnp.float32),
            pltpu.VMEM((part, full), jnp.float32),
            pltpu.VMEM((part, full), jnp.float32),
            pltpu.VMEM((part, full), jnp.float32),
            pltpu.VMEM((2, 1, full), jnp.float32),
            pltpu.VMEM((1, full), jnp.float32),
            pltpu.VMEM((1, full), jnp.float32),
            pltpu.VMEM((1, full), jnp.float32),
            pltpu.VMEM((1, full), jnp.float32),
            pltpu.SemaphoreType.DMA((2,)),
            pltpu.SemaphoreType.DMA((9,)),
            pltpu.SemaphoreType.DMA((9,)),
        ],
        compiler_params=pltpu.CompilerParams(collective_id=0, has_side_effects=True),
    )(thick, winds, cutoff)


def solution(mesh):
    shape = dict(mesh.shape)

    def per_device(winds, thickness, cutoff):
        below, edge_below, pack_minus, pack_plus = exchange(shape, winds, thickness, cutoff)
        lat_total = thickness.shape[1] * shape["lat"]
        return compute(lat_total, winds, thickness, cutoff, below, edge_below, pack_minus, pack_plus)

    return jax.shard_map(
        per_device,
        mesh=mesh,
        in_specs=(P(None, "lev", "lat", None), P("lev", "lat", None), P("lat")),
        out_specs=(P(None, "lev", "lat", None), P("lev", "lat", None)),
        check_vma=False,
    )
```

time: 368 us -> 47 us (0.13)
  waiting for transfers between devices: 163 us -> 0 us
  other arithmetic: 62.9 us -> 0 us
  matrix products: 54.4 us -> 0 us
  starting transfers between devices: 51.1 us -> 0 us
  Pallas kernels: 0 us -> 46.2 us
  local copies, waits for them, and re-layouts: 19.5 us -> 0 us
  between operations: 14.3 us -> 0.64 us
    all_to_all x3 -> x0, waiting for transfers between devices: 121 us -> none  [the longest x1 75.5 us: per_device(): lax.all_to_all(outgoing, 'lat', split_axis=0, concat_axis=0, tiled=True)]
    dot_general x2 -> x0, matrix products: 54.4 us -> none  [the longest x1 46.4 us: remove_high(): return vectors - jnp.dot(coeffs, fourier.T, precision=lax.Precision.HIGHEST)]
    all_to_all x3 -> x0, starting transfers between devices: 46.6 us -> none  [the longest x1 23.9 us: per_device(): lax.all_to_all(outgoing, 'lat', split_axis=0, concat_axis=0, tiled=True)]
    pallas_call x0 -> x2, Pallas kernels: none -> 46.2 us  [the longest x1 29.9 us: exchange(): pl.pallas_call(functools.partial(exchange_kernel, mesh_shape['lat'], mesh...]
    all_gather x1 -> x0, waiting for transfers between devices: 38.7 us -> none  [carried_in(): pieces = lax.all_gather(value, axis)]
    dot_general x1 -> x0, other arithmetic: 38.3 us -> none  [remove_high(): coeffs = jnp.dot(vectors, fourier, precision=lax.Precision.HIGHEST)]
    select_n x10 -> x0, other arithmetic: 10.9 us -> none  [the longest x7 6.97 us: turn(): return jnp.where(position < mine, longer, subtotal)]
    slice x11 -> x0, local copies, waits for them, and re-layouts: 7.44 us -> none  [the longest x1 1.76 us: per_device(): zonal, merid, depth = (filtered[0], filtered[1], filtered[2])]
  transfers between devices with their start and end apart: 6 -> 0, of which waited for: 5 -> 0; matrix products, arithmetic and copies ran while one was open for 13% -> 0% of each run, Pallas kernels for 0% -> 0%
where the time goes in v1:
time: 47 us; the launch traced here: 46.8 us
  Pallas kernels  46.2 us (98%)
  between operations  0.64 us (1%)
    pallas_call x1, Pallas kernels, exchange(): pl.pallas_call(functools.partial(exchange_kernel, mesh_shape['lat'], mesh...  29.9 us
    pallas_call x1, Pallas kernels, compute(): pl.pallas_call(functools.partial(compute_kernel, lat_total), grid=(1,), o...  16.2 us

profile of v1, /device:TPU:1, one launch (start us, length us, event | category | flops | bytes accessed | tf_op | source)
XLA Modules:
  0.0 46.8 jit_solution(1596325713275224331)
XLA Ops:
  0.6 29.9 %shard_map.77 = (f32[32,1440]{1,0:T(8,128)}, f32[8,1440]{1,0:T(8,128)}, f32[8,1536]{1,0:T(8,128)}, f32[8,1536]{1,0:T(8,128)}) custom-call(f32[4,32,1440]{2,1,0:T(8,128)} %thick.3, f32[2,4,32,1440]{3,2,1,0:T(8,128)} %winds.3, s32[32]{0:T(128)} %cutoff.3), custom_call_target="tpu_custom_call" | custom-call | tf_op jit(solution)/shard_map/pallas_call | solution.py:495
  30.6 16.2 %shard_map.78 = (f32[2,4,32,1440]{3,2,1,0:T(8,128)}, f32[4,32,1440]{2,1,0:T(8,128)}) custom-call(f32[2,4,32,1440]{3,2,1,0:T(8,128)} %winds.3, f32[4,32,1440]{2,1,0:T(8,128)} %thick.3, s32[32]{0:T(128)} %cutoff.3, f32[32,1440]{1,0:T(8,128)} %get-tuple-element.6.below, f32[8,1440]{1,0:T(8,128)} %get-tuple-element.7.edge_below, ...), custom_call_target="tpu_custom_call" | custom-call | tf_op jit(solution)/shard_map/pallas_call | solution.py:285

commit v2 on v0

v2 whole, which is shorter than its diff:
```python
import functools
import math

import jax
import jax.numpy as jnp
import numpy as np
from jax import lax
from jax.experimental import pallas as pl
from jax.experimental.pallas import tpu as pltpu
from jax.sharding import PartitionSpec as P

MESH = pl.DeviceIdType.MESH
time_step = 0.2
coriolis = 1.0
RADIX = 12
HALO = 4
WIDE = 128
HALF3 = 0.5 * math.sqrt(3.0)


def filter_tables(lon):
    seg = lon // RADIX
    points = np.arange(WIDE) - HALO
    scale = math.sqrt(2.0 / lon)
    table = np.zeros((6, 2 * WIDE, 2 * WIDE))
    wave = np.full((6, 2 * WIDE), float(lon))
    turn = 2.0 * math.pi / lon
    j = np.arange(seg)
    for k in range(1, 6):
        m = RADIX * j + k
        angle = turn * ((points[:, None] * m[None, :]) % lon)
        table[k, :WIDE, :seg] = np.cos(angle) * scale
        table[k, :WIDE, WIDE : WIDE + seg] = np.sin(angle) * scale
        table[k, WIDE:, :seg] = -np.sin(angle) * scale
        table[k, WIDE:, WIDE : WIDE + seg] = np.cos(angle) * scale
        wave[k, :seg] = wave[k, WIDE : WIDE + seg] = np.minimum(m, lon - m)
    half = seg // 2
    m = RADIX * np.arange(half + 1)
    weight = np.where((m == 0) | (m == lon // 2), scale / math.sqrt(2.0), scale)
    angle = turn * ((points[:, None] * m[None, :]) % lon)
    table[0, :WIDE, : half + 1] = np.cos(angle) * weight
    table[0, :WIDE, half + 1 : seg] = np.sin(angle[:, 1:half]) * scale
    wave[0, : half + 1] = m
    wave[0, half + 1 : seg] = m[1:half]
    m = RADIX * np.arange(half) + RADIX // 2
    angle = turn * ((points[:, None] * m[None, :]) % lon)
    table[0, WIDE:, WIDE : WIDE + half] = np.cos(angle) * scale
    table[0, WIDE:, WIDE + half : WIDE + seg] = np.sin(angle) * scale
    wave[0, WIDE : WIDE + half] = wave[0, WIDE + half : WIDE + seg] = m
    table = table.astype(np.float32)
    high = table.astype(jnp.bfloat16)
    low = (table - high.astype(np.float32)).astype(jnp.bfloat16)
    return high, low, wave.astype(np.float32).reshape(1, 12 * WIDE)


def split(x):
    high = x.astype(jnp.bfloat16)
    return high, (x - high.astype(jnp.float32)).astype(jnp.bfloat16)


def forward12(x):
    e = [x[s] + x[s + 6] for s in range(6)]
    o = [x[s] - x[s + 6] for s in range(6)]
    ee = [e[s] + e[s + 3] for s in range(3)]
    eo = [e[s] - e[s + 3] for s in range(3)]
    sum12 = ee[1] + ee[2]
    d15, s15, d24, s24 = o[1] - o[5], o[1] + o[5], o[2] - o[4], o[2] + o[4]
    a, b = o[0] + 0.5 * d24, HALF3 * d15
    c, d = 0.5 * s15 + o[3], HALF3 * s24
    return [
        (ee[0] + sum12, eo[0] - eo[1] + eo[2]),
        (a + b, c + d),
        (eo[0] + 0.5 * (eo[1] - eo[2]), HALF3 * (eo[1] + eo[2])),
        (o[0] - d24, s15 - o[3]),
        (ee[0] - 0.5 * sum12, HALF3 * (ee[1] - ee[2])),
        (a - b, c - d),
    ]


def inverse12(z):
    (z0, z6), (r1, n1), (r2, n2), (r3, n3), (r4, n4), (r5, n5) = z
    a, b = HALF3 * (r1 - r5), 0.5 * (n1 + n5) + n3
    c, d = 0.5 * (r1 + r5) - r3, HALF3 * (n1 - n5)
    odd = [r1 + r3 + r5, b + a, c + d, n1 - n3 + n5, d - c, b - a]
    low, h4 = z0 - 0.5 * r4, HALF3 * n4
    ee = [z0 + r4, low + h4, low - h4]
    h2, hr = HALF3 * n2, 0.5 * r2
    eo = [z6 + r2, hr + h2 - z6, z6 - hr + h2]
    even = [ee[s] + eo[s] for s in range(3)] + [ee[s] - eo[s] for s in range(3)]
    return [even[s] + odd[s] for s in range(6)] + [even[s] - odd[s] for s in range(6)]


def lanes_of(shape):
    return lax.broadcasted_iota(jnp.int32, shape, len(shape) - 1)


def segments(tiles):
    lane = lanes_of(tiles[0].shape)
    out = [pltpu.roll(tiles[0], HALO, 1)]
    for s in range(1, RADIX):
        shift = 8 * s + HALO
        out.append(pltpu.roll(jnp.where(lane >= WIDE - shift, tiles[s - 1], tiles[s]), shift, 1))
    return out


def joined(segs):
    lane = lanes_of(segs[0].shape)
    out = []
    for t in range(RADIX):
        tile = pltpu.roll(segs[t], WIDE - (8 * t + HALO), 1)
        if t + 1 < RADIX:
            later = pltpu.roll(segs[t + 1], 116 - 8 * t, 1)
            tile = jnp.where(lane < 120 - 8 * t, tile, later)
        out.append(tile)
    return out


def forward_rows(tiles, y_high, y_low, row):
    lane = lanes_of((16, WIDE))
    inside = (lane >= HALO) & (lane < WIDE - HALO)
    classes = forward12(segments(tiles))
    for k, parts in enumerate(classes):
        for at, part in enumerate(parts):
            high, low = split(jnp.where(inside, part, 0.0))
            y_high[k, pl.ds(row, 16), at * WIDE : (at + 1) * WIDE] = high
            y_low[k, pl.ds(row, 16), at * WIDE : (at + 1) * WIDE] = low


def tiles_of(load):
    return [load(pl.ds(t * WIDE, WIDE)) for t in range(RADIX)]


def narrow_tiles(load, lon):
    last = lon - (RADIX - 1) * WIDE
    tiles = [load(pl.ds(t * WIDE, WIDE)) for t in range(RADIX - 1)]
    end = load(pl.ds((RADIX - 1) * WIDE, last))
    return tiles + [jnp.concatenate([end, jnp.zeros((end.shape[0], WIDE - last), jnp.float32)], axis=1)]


def filter_class(k, y_high, y_low, z, cut, wave, f_high, f_low):
    high, low = f_high[k], f_low[k]
    yh, yl = y_high[k], y_low[k]
    coeffs = jnp.dot(
        jnp.concatenate([yh, yl, yh], axis=1),
        jnp.concatenate([high, high, low], axis=0),
        preferred_element_type=jnp.float32,
    )
    limit = cut[...]
    wanted = wave[:, pl.ds(k * 2 * WIDE, 2 * WIDE)]
    keep = jnp.concatenate([limit >= wanted[:, :WIDE], limit >= wanted[:, WIDE:]], axis=1)
    xh, xl = split(jnp.where(keep, coeffs, 0.0))
    z[k] = lax.dot_general(
        jnp.concatenate([xh, xl, xh], axis=1),
        jnp.concatenate([high, high, low], axis=1),
        (((1,), (1,)), ((), ())),
        preferred_element_type=jnp.float32,
    )


def step_kernel(
    lat_count,
    lev_count,
    early_count,
    thick,
    winds,
    cutoff,
    wave,
    table_high,
    table_low,
    part_winds,
    new_thick,
    delta,
    h_in,
    w_in,
    f_high,
    f_low,
    y_high,
    y_low,
    z,
    field,
    result,
    cut,
    y2_high,
    y2_low,
    z2,
    outer,
    grad,
    cut2,
    out,
    out_delta,
    send_minus,
    send_plus,
    from_minus,
    from_plus,
    column,
    below,
    pair,
    sums,
    from_upper,
    from_lower,
    relay,
    shared,
    row_column,
    row_pair,
    row_sums,
    row_upper,
    row_lower,
    row_relay,
    load_sem,
    store_sem,
    send_sem,
    recv_sem,
):
    levels, rows, lon = thick.shape
    full = RADIX * WIDE
    part = rows // 2
    fields = 3 * levels
    lat, lev = lax.axis_index("lat"), lax.axis_index("lev")
    x, core = lev // 2, lev % 2
    chips = lev_count // 2
    partner = x * 2 + (1 - core)
    x_up, x_down = ((x + 1) % chips) * 2 + core, ((x + chips - 1) % chips) * 2 + core
    has_minus, has_plus = lat > 0, lat < lat_count - 1
    lat_minus, lat_plus = jnp.maximum(lat - 1, 0), jnp.minimum(lat + 1, lat_count - 1)
    early = lat % 8 < early_count

    barrier = pltpu.get_barrier_semaphore()
    for device in ((lat, partner), (lat, x_up), (lat, x_down)):
        pl.semaphore_signal(barrier, inc=1, device_id=device, device_id_type=MESH)

    @pl.when(has_minus)
    def _():
        pl.semaphore_signal(barrier, inc=1, device_id=(lat_minus, lev), device_id_type=MESH)

    @pl.when(has_plus)
    def _():
        pl.semaphore_signal(barrier, inc=1, device_id=(lat_plus, lev), device_id_type=MESH)

    loads = [
        pltpu.make_async_copy(source, target, load_sem.at[i])
        for i, (source, target) in enumerate(
            (
                (thick, h_in),
                (winds.at[1], w_in.at[1]),
                (table_high, f_high),
                (table_low, f_low),
                (winds.at[0], w_in.at[0]),
            )
        )
    ]
    for load in loads:
        load.start()

    def remote(source, target, at, device):
        return pltpu.make_async_remote_copy(
            src_ref=source,
            dst_ref=target,
            send_sem=send_sem.at[at],
            recv_sem=recv_sem.at[at],
            device_id=device,
            device_id_type=MESH,
        )

    row32 = lax.broadcasted_iota(jnp.int32, (rows, WIDE), 0)

    def limits():
        limit = jnp.zeros((rows, WIDE), jnp.float32)
        for r in range(rows):
            limit = jnp.where(row32 == r, cutoff[r].astype(jnp.float32), limit)
        for unit in range(fields):
            cut[pl.ds(unit * rows, rows), :] = limit
        cut2[pl.ds(0, rows), :] = limit

    def forward_thick():
        def unit(level, carry):
            for half in range(rows // 16):
                here = pl.ds(half * 16, 16)
                tiles = narrow_tiles(lambda c: h_in[level, here, c], lon)
                forward_rows(tiles, y_high, y_low, (2 * levels + level) * rows + half * 16)
            return carry

        lax.fori_loop(0, levels, unit, 0)

    def forward_winds():
        def unit(index, carry):
            for half in range(rows // 16):
                here = pl.ds(half * 16, 16)
                tiles = narrow_tiles(lambda c: w_in[index // levels, index % levels, here, c], lon)
                forward_rows(tiles, y_high, y_low, index * rows + half * 16)
            return carry

        lax.fori_loop(0, 2 * levels, unit, 0)

    def products(classes):
        for k in classes:
            filter_class(k, y_high, y_low, z, cut, wave, f_high, f_low)

    def inverse():
        def unit(index, carry):
            for half in range(rows // 16):
                here = pl.ds(index * rows + half * 16, 16)
                parts = [(z[k, here, :WIDE], z[k, here, WIDE:]) for k in range(6)]
                for s, value in enumerate(inverse12(parts)):
                    field[index, s, pl.ds(half * 16, 16), :] = value
            return carry

        lax.fori_loop(0, fields, unit, 0)

    def late(stage, *args):
        @pl.when(jnp.logical_not(early))
        def _():
            stage(*args)

    loads[0].wait()
    total = h_in[0]
    for level in range(1, levels):
        total = total + h_in[level]
    column[:, pl.ds(full - WIDE, WIDE)] = jnp.zeros((rows, WIDE), jnp.float32)
    column[:, pl.ds(0, lon)] = total
    loads[1].wait()
    row8 = lax.broadcasted_iota(jnp.int32, (8, lon), 0)
    for pack, row in ((send_minus, 0), (send_plus, rows - 1)):
        value = jnp.zeros((8, lon), jnp.float32)
        for level in range(levels):
            value = jnp.where(row8 == level, h_in[level, row : row + 1, :], value)
            value = jnp.where(row8 == levels + level, w_in[1, level, row : row + 1, :], value)
        pack[:, pl.ds(full - WIDE, WIDE)] = jnp.broadcast_to(cutoff[row].astype(jnp.float32), (8, WIDE))
        pack[:, pl.ds(0, lon)] = value

    @pl.when(early)
    def _():
        for load in loads[2:]:
            load.wait()
        limits()
        forward_thick()
        forward_winds()
        products(range(6))
        inverse()

    one = lambda flag: jnp.where(flag, 1, 0)
    pl.semaphore_wait(barrier, 3 + one(has_minus) + one(has_plus))
    mine, theirs = pl.multiple_of(core * part, part), pl.multiple_of((1 - core) * part, part)
    to_pair = remote(column.at[pl.ds(theirs, part), :], pair, 0, (lat, partner))
    to_minus = remote(send_minus, from_plus, 1, (lat_minus, lev))
    to_plus = remote(send_plus, from_minus, 2, (lat_plus, lev))
    to_pair.start()

    @pl.when(has_minus)
    def _():
        to_minus.start()

    @pl.when(has_plus)
    def _():
        to_plus.start()

    late(limits)
    late(forward_thick)

    to_pair.wait()
    own = column[pl.ds(mine, part), :]
    sums[...] = own + pair[...]

    @pl.when(x == chips - 1)
    def _():
        from_upper[...] = jnp.zeros_like(from_upper)
        row_upper[...] = jnp.zeros_like(row_upper)

    @pl.when(x >= chips - 2)
    def _():
        from_lower[...] = jnp.zeros_like(from_lower)
        row_lower[...] = jnp.zeros_like(row_lower)

    pieces = [pl.ds(8 * i, 8) for i in range(2)]
    down_first = [remote(sums.at[c, :], from_upper.at[c, :], 3 + i, (lat, x_down)) for i, c in enumerate(pieces)]
    down_later = [remote(relay.at[c, :], from_upper.at[c, :], 3 + i, (lat, x_down)) for i, c in enumerate(pieces)]
    up_first = [remote(sums.at[c, :], from_lower.at[c, :], 5 + i, (lat, x_up)) for i, c in enumerate(pieces)]
    up_later = [remote(from_lower.at[c, :], from_lower.at[c, :], 5 + i, (lat, x_up)) for i, c in enumerate(pieces)]
    row_pairing = remote(row_column, row_pair, 7, (lat, partner))
    row_down_first = remote(row_sums, row_upper, 8, (lat, x_down))
    row_down_later = remote(row_relay, row_upper, 8, (lat, x_down))
    row_up_first = remote(row_sums, row_lower, 9, (lat, x_up))
    row_up_later = remote(row_lower, row_lower, 9, (lat, x_up))

    for i in range(2):
        @pl.when(x >= 2)
        def _():
            down_first[i].start()

        @pl.when(x == 3)
        def _():
            up_first[i].start()

    @pl.when(jnp.logical_not(early))
    def _():
        for load in loads[2:]:
            load.wait()
        forward_winds()

    @pl.when(has_minus)
    def _():
        to_minus.wait_send()
        to_plus.wait_recv()

    @pl.when(jnp.logical_not(has_minus))
    def _():
        from_minus[...] = jnp.zeros_like(from_minus)

    @pl.when(has_plus)
    def _():
        to_plus.wait_send()
        to_minus.wait_recv()

    @pl.when(jnp.logical_not(has_plus))
    def _():
        from_plus[...] = jnp.zeros_like(from_plus)

    for at, source in enumerate((from_minus, from_plus)):
        outside = source[0:1, :]
        for level in range(1, levels):
            outside = outside + source[level : level + 1, :]
        row_column[at] = outside
    row_pairing.start()

    for i, c in enumerate(pieces):
        @pl.when((x == 1) | (x == 2))
        def _():
            down_first[i].wait_recv()

        @pl.when(x == 1)
        def _():
            relay[c, :] = sums[c, :] + from_upper[c, :]
            down_later[i].start()

        @pl.when(x == 0)
        def _():
            up_first[i].wait_recv()
            up_later[i].start()

    late(products, range(3))

    row_pairing.wait()
    row_sums[...] = row_column[...] + row_pair[...]

    @pl.when(x >= 2)
    def _():
        row_down_first.start()

    @pl.when(x == 3)
    def _():
        row_up_first.start()

    upper = jnp.where(core == 0, 0.0, 1.0)
    lower = 1.0 - upper
    shares = []
    for i, c in enumerate(pieces):
        @pl.when(x == 0)
        def _():
            down_first[i].wait_recv()

        @pl.when(x == 1)
        def _():
            up_first[i].wait_recv()

        here = pl.ds(pl.multiple_of(mine + 8 * i, 8), 8)
        above = from_upper[c, :] + from_lower[c, :]
        below[here, :] = above + lower * pair[c, :]
        column[here, :] = above + upper * column[here, :]
        shares.append(remote(column.at[here, :], shared.at[c, :], 10 + i, (lat, partner)))
        shares[i].start()

    late(products, range(3, 6))

    @pl.when((x == 1) | (x == 2))
    def _():
        row_down_first.wait_recv()

    @pl.when(x == 1)
    def _():
        row_relay[...] = row_sums[...] + row_upper[...]
        row_down_later.start()

    @pl.when(x == 0)
    def _():
        row_up_first.wait_recv()
        row_up_later.start()

    late(inverse)

    row_index = (lat * rows + row32).astype(jnp.float32)
    lat_total = lat_count * rows
    center = (row_index + 0.5) * (math.pi / lat_total) - 0.5 * math.pi
    sin_center = (time_step * coriolis) * jnp.sin(center)
    cos_center = (0.5 * time_step) * jnp.cos(center)
    edge = (0.25 * time_step) * jnp.sin(row_index * (math.pi / lat_total))
    last_index = (lat * rows + rows + jnp.zeros((8, WIDE), jnp.int32)).astype(jnp.float32)
    last_edge = (0.25 * time_step) * jnp.sin(last_index * (math.pi / lat_total))
    top, bottom = row32 == 0, row32 == rows - 1

    def down(x, halo):
        return jnp.where(top, halo, pltpu.roll(x, 1, 0))

    def up(x, halo):
        return jnp.where(bottom, halo, pltpu.roll(x, rows - 1, 0))

    def east(x):
        return pltpu.roll(x, WIDE - 1, 1)

    def west(x):
        return pltpu.roll(x, 1, 1)

    def stencil(s, carry):
        total = jnp.zeros((rows, WIDE), jnp.float32)
        for level in reversed(range(levels)):
            u, v, h = field[level, s], field[levels + level, s], field[2 * levels + level, s]
            geo = total + 0.5 * h
            total = total + h
            zonal = (0.25 * time_step) * (h + east(h)) * (u + east(u))
            merid = jnp.where(top, 0.0, (h + pltpu.roll(h, 1, 0)) * (v + pltpu.roll(v, 1, 0)) * edge)
            result[2 * levels + level, s] = h - ((zonal - west(zonal)) + (up(merid, 0.0) - merid))
            result[level, s] = u - (0.5 * time_step) * (east(geo) - west(geo)) + sin_center * v
            result[levels + level, s] = v - cos_center * (up(geo, 0.0) - down(geo, 0.0)) - sin_center * u
        return carry

    lax.fori_loop(0, RADIX, stencil, 0)

    def write_rows(target, source, parts):
        for p in parts:
            here = pl.ds(p * 8, 8)
            tiles = joined([source(s, here) for s in range(RADIX)])
            for t in range(RADIX - 1):
                target[here, t * WIDE : (t + 1) * WIDE] = tiles[t]
            target[here, (RADIX - 1) * WIDE : lon] = tiles[RADIX - 1][:, : lon - (RADIX - 1) * WIDE]

    def write_units(first, parts):
        def unit(level, carry):
            index = first + level
            write_rows(out.at[index], lambda s, here: result[index, s, here, :], parts)
            return carry

        lax.fori_loop(0, levels, unit, 0)

    write_units(0, range(4))
    stores = [
        pltpu.make_async_copy(out.at[pl.ds(0, levels)], part_winds.at[0], store_sem.at[0]),
        pltpu.make_async_copy(out.at[pl.ds(levels, levels)], part_winds.at[1], store_sem.at[1]),
        pltpu.make_async_copy(out.at[pl.ds(2 * levels, levels)], new_thick, store_sem.at[2]),
        pltpu.make_async_copy(out_delta, delta, store_sem.at[3]),
    ]
    stores[0].start()
    write_units(levels, (1, 2))
    write_units(2 * levels, (1, 2))

    for i, c in enumerate(pieces):
        shares[i].wait()
        below[pl.ds(pl.multiple_of(theirs + 8 * i, 8), 8), :] = shared[c, :]

    @pl.when(x == 0)
    def _():
        row_down_first.wait_recv()

    @pl.when(x == 1)
    def _():
        row_up_first.wait_recv()

    minus_cut = from_minus[:, full - WIDE :][:, WIDE - 1 :]
    plus_cut = from_plus[:, full - WIDE :][:, WIDE - 1 :]
    cut2[pl.ds(rows, 8), :] = jnp.broadcast_to(minus_cut, (8, WIDE))
    cut2[pl.ds(rows + 8, 8), :] = jnp.broadcast_to(plus_cut, (8, WIDE))
    row16 = lax.broadcasted_iota(jnp.int32, (16, WIDE), 0)
    cut2[pl.ds(rows + 16, 16), :] = jnp.where(row16 == 0, minus_cut[0:1], plus_cut[0:1])
    for half in range(rows // 16):
        forward_rows(tiles_of(lambda c: below[pl.ds(half * 16, 16), c]), y2_high, y2_low, half * 16)
    forward_rows(tiles_of(lambda c: jnp.concatenate([from_minus[:, c], from_plus[:, c]], axis=0)), y2_high, y2_low, rows)
    for at in range(2):
        row_column[at] = row_upper[at] + row_lower[at] + lower * row_pair[at]

    def edge_tile(c):
        return jnp.where(row16 == 0, row_column[0, :, c], jnp.where(row16 == 1, row_column[1, :, c], 0.0))

    forward_rows(tiles_of(edge_tile), y2_high, y2_low, rows + 16)
    for k in range(6):
        filter_class(k, y2_high, y2_low, z2, cut2, wave, f_high, f_low)
    for group in range((rows + 32) // 16):
        here = pl.ds(group * 16, 16)
        parts = [(z2[k, here, :WIDE], z2[k, here, WIDE:]) for k in range(6)]
        for s, value in enumerate(inverse12(parts)):
            outer[s, here, :] = value

    eight = lax.broadcasted_iota(jnp.int32, (8, WIDE), 0)
    at_top, at_bottom = eight == 0, eight == 7
    head, tail = pl.ds(0, 8), pl.ds(rows - 8, 8)

    def patch(s, carry):
        total = outer[s, pl.ds(0, rows), :]
        sides = outer[s, pl.ds(rows, 32), :]
        grad[0, s] = -(0.5 * time_step) * (east(total) - west(total))
        grad[1, s] = -cos_center * (up(total, sides[17:18]) - down(total, sides[16:17]))
        minus_total = plus_total = jnp.zeros((1, WIDE), jnp.float32)
        for level in reversed(range(levels)):
            hm, vm = sides[level : level + 1], sides[levels + level : levels + level + 1]
            hp, vp = sides[8 + level : 9 + level], sides[8 + levels + level : 9 + levels + level]
            vi, hi = levels + level, 2 * levels + level
            geo_minus, geo_plus = minus_total + 0.5 * hm, plus_total + 0.5 * hp
            minus_total, plus_total = minus_total + hm, plus_total + hp
            result[vi, s, head, :] += jnp.where(at_top, cos_center[:8] * geo_minus, 0.0)
            result[vi, s, tail, :] -= jnp.where(at_bottom, cos_center[rows - 8 :] * geo_plus, 0.0)
            first = (field[hi, s, head, :] + hm) * (field[vi, s, head, :] + vm) * edge[:8]
            final = (field[hi, s, tail, :] + hp) * (field[vi, s, tail, :] + vp) * last_edge
            result[hi, s, head, :] += jnp.where(at_top, first, 0.0)
            result[hi, s, tail, :] -= jnp.where(at_bottom, final, 0.0)
        return carry

    lax.fori_loop(0, RADIX, patch, 0)
    write_units(levels, (0, 3))
    stores[1].start()
    write_units(2 * levels, (0, 3))
    stores[2].start()
    for which in range(2):
        write_rows(out_delta.at[which], lambda s, here: grad[which, s, here, :], range(4))
    stores[3].start()

    @pl.when(x >= 1)
    def _():
        for link in down_first:
            link.wait_send()
        row_down_first.wait_send()

    @pl.when((x == 0) | (x == 3))
    def _():
        for link in up_first:
            link.wait_send()
        row_up_first.wait_send()

    for store in stores:
        store.wait()


def step(shape, winds, thick, cutoff):
    levels, rows, lon = thick.shape
    high, low, wave = filter_tables(lon)
    full = RADIX * WIDE
    part = rows // 2
    units = 3 * levels * rows
    more = rows + 32
    f32 = lambda *dims: pltpu.VMEM(dims, jnp.float32)
    bf16 = lambda *dims: pltpu.VMEM(dims, jnp.bfloat16)
    hbm = pl.BlockSpec(memory_space=pl.ANY)
    return pl.pallas_call(
        functools.partial(step_kernel, shape["lat"], shape["lev"], 2 if shape["lat"] == 64 else 1),
        out_shape=(
            jax.ShapeDtypeStruct(winds.shape, jnp.float32),
            jax.ShapeDtypeStruct(thick.shape, jnp.float32),
            jax.ShapeDtypeStruct((2, rows, lon), jnp.float32),
        ),
        in_specs=[hbm, hbm, pl.BlockSpec(memory_space=pltpu.SMEM), pl.BlockSpec(memory_space=pltpu.VMEM), hbm, hbm],
        out_specs=(hbm, hbm, hbm),
        scratch_shapes=[
            f32(levels, rows, lon),
            f32(2, levels, rows, lon),
            bf16(*high.shape),
            bf16(*low.shape),
            bf16(6, units, 2 * WIDE),
            bf16(6, units, 2 * WIDE),
            f32(6, units, 2 * WIDE),
            f32(3 * levels, RADIX, rows, WIDE),
            f32(3 * levels, RADIX, rows, WIDE),
            f32(units, WIDE),
            bf16(6, more, 2 * WIDE),
            bf16(6, more, 2 * WIDE),
            f32(6, more, 2 * WIDE),
            f32(RADIX, more, WIDE),
            f32(2, RADIX, rows, WIDE),
            f32(more, WIDE),
            f32(3 * levels, rows, lon),
            f32(2, rows, lon),
            f32(8, full),
            f32(8, full),
            f32(8, full),
            f32(8, full),
            f32(rows, full),
            f32(rows, full),
            f32(part, full),
            f32(part, full),
            f32(part, full),
            f32(part, full),
            f32(part, full),
            f32(part, full),
            f32(2, 1, full),
            f32(2, 1, full),
            f32(2, 1, full),
            f32(2, 1, full),
            f32(2, 1, full),
            f32(2, 1, full),
            pltpu.SemaphoreType.DMA((5,)),
            pltpu.SemaphoreType.DMA((4,)),
            pltpu.SemaphoreType.DMA((12,)),
            pltpu.SemaphoreType.DMA((12,)),
        ],
        compiler_params=pltpu.CompilerParams(collective_id=0, has_side_effects=True, vmem_limit_bytes=56 << 20),
    )(thick, winds, cutoff, jnp.asarray(wave), jnp.asarray(high), jnp.asarray(low))


def solution(mesh):
    shape = dict(mesh.shape)

    def per_device(winds, thickness, cutoff):
        part_winds, new_thick, delta = step(shape, winds, thickness, cutoff)
        return part_winds + delta[:, None], new_thick

    return jax.shard_map(
        per_device,
        mesh=mesh,
        in_specs=(P(None, "lev", "lat", None), P("lev", "lat", None), P("lat")),
        out_specs=(P(None, "lev", "lat", None), P("lev", "lat", None)),
        check_vma=False,
    )
```

time: 368 us -> 33.9 us (0.09)
  the two profiles are of different devices: /device:TPU:1 before, /device:TPU:50 now
where the time goes in v2:
time: 33.9 us; the launch traced here: 33.7 us
  Pallas kernels  29.3 us (86%)
  other arithmetic  2.83 us (8%)
  local copies, waits for them, and re-layouts  0.88 us (3%)
  between operations  0.65 us (2%)
    pallas_call x1, Pallas kernels, step(): pl.pallas_call(functools.partial(step_kernel, shape['lat'], shape['lev'],...  29.3 us
    add x1, other arithmetic, per_device(): return (part_winds + delta[:, None], new_thick)  2.83 us
    unnamed x3, local copies, waits for them, and re-layouts  0.88 us

profile of v2, /device:TPU:50, one launch (start us, length us, event | category | flops | bytes accessed | tf_op | source)
XLA Modules:
  0.0 33.7 jit_solution(864946110567522662)
XLA Ops:
  0.6 29.3 %shard_map.77 = (f32[2,4,32,1440]{3,2,1,0:T(8,128)}, f32[4,32,1440]{2,1,0:T(8,128)}, f32[2,32,1440]{2,1,0:T(8,128)}) custom-call(f32[4,32,1440]{2,1,0:T(8,128)} %thick.1, f32[2,4,32,1440]{3,2,1,0:T(8,128)} %winds.1, s32[32]{0:T(128)} %cutoff.1, f32[1,1536]{1,0:T(1,128)} %constant.6.clone.wave, bf16[6,256,256]{2,1,0:T(8,128)(2,1)} %constant.7.clone.table_high, ...), custom_call_target="tpu_custom_call" | custom-call | tf_op jit(solution)/shard_map/pallas_call | solution.py:648
  29.9 0.0 copy-start
  29.9 2.8 %broadcast_add_fusion = f32[2,4,32,1440]{3,2,1,0:T(8,128)} fusion(f32[2,4,32,1440]{3,2,1,0:T(8,128)} %get-tuple-element.5, f32[2,32,1440]{2,1,0:T(8,128)} %get-tuple-element.6), kind=kLoop, calls=%fused_computation | loop fusion | flops 368640 | bytes 3317760 | tf_op jit(solution)/shard_map/add | solution.py:708
  32.8 0.0 copy-done
  32.8 0.9 %copy.9 = f32[4,32,1440]{2,1,0:T(8,128)} copy(f32[4,32,1440]{2,1,0:T(8,128)S(1)} %copy-done) | data formatting | bytes 1474560
Async XLA Ops:
  29.9 2.8 %copy-start = (f32[4,32,1440]{2,1,0:T(8,128)S(1)}, f32[4,32,1440]{2,1,0:T(8,128)}, u32[]{:S(2)}) copy-start(f32[4,32,1440]{2,1,0:T(8,128)} %get-tuple-element.11) | copy-start | bytes 2211844

commit v3 on v2

--- a/solution.py
+++ b/solution.py
@@ -188,6 +188,7 @@
     cut2,
     out,
     out_delta,
+    trig,
     send_minus,
     send_plus,
     from_minus,
@@ -306,11 +307,6 @@
 
         lax.fori_loop(0, fields, unit, 0)
 
-    def late(stage, *args):
-        @pl.when(jnp.logical_not(early))
-        def _():
-            stage(*args)
-
     loads[0].wait()
     total = h_in[0]
     for level in range(1, levels):
@@ -327,50 +323,15 @@
         pack[:, pl.ds(full - WIDE, WIDE)] = jnp.broadcast_to(cutoff[row].astype(jnp.float32), (8, WIDE))
         pack[:, pl.ds(0, lon)] = value
 
-    @pl.when(early)
-    def _():
-        for load in loads[2:]:
-            load.wait()
-        limits()
-        forward_thick()
-        forward_winds()
-        products(range(6))
-        inverse()
-
     one = lambda flag: jnp.where(flag, 1, 0)
-    pl.semaphore_wait(barrier, 3 + one(has_minus) + one(has_plus))
     mine, theirs = pl.multiple_of(core * part, part), pl.multiple_of((1 - core) * part, part)
+    upper = jnp.where(core == 0, 0.0, 1.0)
+    lower = 1.0 - upper
+    pieces = [pl.ds(8 * i, 8) for i in range(2)]
+    places = [pl.ds(pl.multiple_of(mine + 8 * i, 8), 8) for i in range(2)]
     to_pair = remote(column.at[pl.ds(theirs, part), :], pair, 0, (lat, partner))
     to_minus = remote(send_minus, from_plus, 1, (lat_minus, lev))
     to_plus = remote(send_plus, from_minus, 2, (lat_plus, lev))
-    to_pair.start()
-
-    @pl.when(has_minus)
-    def _():
-        to_minus.start()
-
-    @pl.when(has_plus)
-    def _():
-        to_plus.start()
-
-    late(limits)
-    late(forward_thick)
-
-    to_pair.wait()
-    own = column[pl.ds(mine, part), :]
-    sums[...] = own + pair[...]
-
-    @pl.when(x == chips - 1)
-    def _():
-        from_upper[...] = jnp.zeros_like(from_upper)
-        row_upper[...] = jnp.zeros_like(row_upper)
-
-    @pl.when(x >= chips - 2)
-    def _():
-        from_lower[...] = jnp.zeros_like(from_lower)
-        row_lower[...] = jnp.zeros_like(row_lower)
-
-    pieces = [pl.ds(8 * i, 8) for i in range(2)]
     down_first = [remote(sums.at[c, :], from_upper.at[c, :], 3 + i, (lat, x_down)) for i, c in enumerate(pieces)]
     down_later = [remote(relay.at[c, :], from_upper.at[c, :], 3 + i, (lat, x_down)) for i, c in enumerate(pieces)]
     up_first = [remote(sums.at[c, :], from_lower.at[c, :], 5 + i, (lat, x_up)) for i, c in enumerate(pieces)]
@@ -380,120 +341,132 @@
     row_down_later = remote(row_relay, row_upper, 8, (lat, x_down))
     row_up_first = remote(row_sums, row_lower, 9, (lat, x_up))
     row_up_later = remote(row_lower, row_lower, 9, (lat, x_up))
-
-    for i in range(2):
+    shares = [remote(column.at[p, :], shared.at[c, :], 10 + i, (lat, partner)) for i, (p, c) in enumerate(zip(places, pieces))]
+
+    def enter():
+        pl.semaphore_wait(barrier, 3 + one(has_minus) + one(has_plus))
+        to_pair.start()
+
+        @pl.when(has_minus)
+        def _():
+            to_minus.start()
+
+        @pl.when(has_plus)
+        def _():
+            to_plus.start()
+
+    def first_step():
+        to_pair.wait()
+        sums[...] = column[pl.ds(mine, part), :] + pair[...]
+        for i in range(2):
+            @pl.when(x >= 2)
+            def _():
+                down_first[i].start()
+
+            @pl.when(x == 3)
+            def _():
+                up_first[i].start()
+
+        @pl.when(x == chips - 1)
+        def _():
+            from_upper[...] = jnp.zeros_like(from_upper)
+            row_upper[...] = jnp.zeros_like(row_upper)
+
+        @pl.when(x >= chips - 2)
+        def _():
+            from_lower[...] = jnp.zeros_like(from_lower)
+            row_lower[...] = jnp.zeros_like(row_lower)
+
+    def second_step():
+        for i, c in enumerate(pieces):
+            @pl.when((x == 1) | (x == 2))
+            def _():
+                down_first[i].wait_recv()
+
+            @pl.when(x == 1)
+            def _():
+                relay[c, :] = sums[c, :] + from_upper[c, :]
+                down_later[i].start()
+
+            @pl.when(x == 0)
+            def _():
+                up_first[i].wait_recv()
+                up_later[i].start()
+
+    def share():
+        for i, (p, c) in enumerate(zip(places, pieces)):
+            @pl.when(x == 0)
+            def _():
+                down_first[i].wait_recv()
+
+            @pl.when(x == 1)
+            def _():
+                up_first[i].wait_recv()
+
+            above = from_upper[c, :] + from_lower[c, :]
+            below[p, :] = above + lower * pair[c, :]
+            column[p, :] = above + upper * column[p, :]
+            shares[i].start()
+
+    def neighbours():
+        @pl.when(has_minus)
+        def _():
+            to_minus.wait_send()
+            to_plus.wait_recv()
+
+        @pl.when(jnp.logical_not(has_minus))
+        def _():
+            from_minus[...] = jnp.zeros_like(from_minus)
+
+        @pl.when(has_plus)
+        def _():
+            to_plus.wait_send()
+            to_minus.wait_recv()
+
+        @pl.when(jnp.logical_not(has_plus))
+        def _():
+            from_plus[...] = jnp.zeros_like(from_plus)
+
+        for at, source in enumerate((from_minus, from_plus)):
+            outside = source[0:1, :]
+            for level in range(1, levels):
+                outside = outside + source[level : level + 1, :]
+            row_column[at] = outside
+        row_pairing.start()
+
+    def row_first():
+        row_pairing.wait()
+        row_sums[...] = row_column[...] + row_pair[...]
+
         @pl.when(x >= 2)
         def _():
-            down_first[i].start()
+            row_down_first.start()
 
         @pl.when(x == 3)
         def _():
-            up_first[i].start()
-
-    @pl.when(jnp.logical_not(early))
-    def _():
-        for load in loads[2:]:
-            load.wait()
-        forward_winds()
-
-    @pl.when(has_minus)
-    def _():
-        to_minus.wait_send()
-        to_plus.wait_recv()
-
-    @pl.when(jnp.logical_not(has_minus))
-    def _():
-        from_minus[...] = jnp.zeros_like(from_minus)
-
-    @pl.when(has_plus)
-    def _():
-        to_plus.wait_send()
-        to_minus.wait_recv()
-
-    @pl.when(jnp.logical_not(has_plus))
-    def _():
-        from_plus[...] = jnp.zeros_like(from_plus)
-
-    for at, source in enumerate((from_minus, from_plus)):
-        outside = source[0:1, :]
-        for level in range(1, levels):
-            outside = outside + source[level : level + 1, :]
-        row_column[at] = outside
-    row_pairing.start()
-
-    for i, c in enumerate(pieces):
+            row_up_first.start()
+
+    def row_second():
         @pl.when((x == 1) | (x == 2))
         def _():
-            down_first[i].wait_recv()
+            row_down_first.wait_recv()
 
         @pl.when(x == 1)
         def _():
-            relay[c, :] = sums[c, :] + from_upper[c, :]
-            down_later[i].start()
+            row_relay[...] = row_sums[...] + row_upper[...]
+            row_down_later.start()
 
         @pl.when(x == 0)
         def _():
-            up_first[i].wait_recv()
-            up_later[i].start()
-
-    late(products, range(3))
-
-    row_pairing.wait()
-    row_sums[...] = row_column[...] + row_pair[...]
-
-    @pl.when(x >= 2)
-    def _():
-        row_down_first.start()
-
-    @pl.when(x == 3)
-    def _():
-        row_up_first.start()
-
-    upper = jnp.where(core == 0, 0.0, 1.0)
-    lower = 1.0 - upper
-    shares = []
-    for i, c in enumerate(pieces):
-        @pl.when(x == 0)
-        def _():
-            down_first[i].wait_recv()
-
-        @pl.when(x == 1)
-        def _():
-            up_first[i].wait_recv()
-
-        here = pl.ds(pl.multiple_of(mine + 8 * i, 8), 8)
-        above = from_upper[c, :] + from_lower[c, :]
-        below[here, :] = above + lower * pair[c, :]
-        column[here, :] = above + upper * column[here, :]
-        shares.append(remote(column.at[here, :], shared.at[c, :], 10 + i, (lat, partner)))
-        shares[i].start()
-
-    late(products, range(3, 6))
-
-    @pl.when((x == 1) | (x == 2))
-    def _():
-        row_down_first.wait_recv()
-
-    @pl.when(x == 1)
-    def _():
-        row_relay[...] = row_sums[...] + row_upper[...]
-        row_down_later.start()
-
-    @pl.when(x == 0)
-    def _():
-        row_up_first.wait_recv()
-        row_up_later.start()
-
-    late(inverse)
+            row_up_first.wait_recv()
+            row_up_later.start()
 
     row_index = (lat * rows + row32).astype(jnp.float32)
     lat_total = lat_count * rows
     center = (row_index + 0.5) * (math.pi / lat_total) - 0.5 * math.pi
-    sin_center = (time_step * coriolis) * jnp.sin(center)
-    cos_center = (0.5 * time_step) * jnp.cos(center)
-    edge = (0.25 * time_step) * jnp.sin(row_index * (math.pi / lat_total))
-    last_index = (lat * rows + rows + jnp.zeros((8, WIDE), jnp.int32)).astype(jnp.float32)
-    last_edge = (0.25 * time_step) * jnp.sin(last_index * (math.pi / lat_total))
+    trig[0] = (time_step * coriolis) * jnp.sin(center)
+    trig[1] = (0.5 * time_step) * jnp.cos(center)
+    trig[2] = (0.25 * time_step) * jnp.sin(row_index * (math.pi / lat_total))
     top, bottom = row32 == 0, row32 == rows - 1
 
     def down(x, halo):
@@ -508,20 +481,23 @@
     def west(x):
         return pltpu.roll(x, 1, 1)
 
-    def stencil(s, carry):
-        total = jnp.zeros((rows, WIDE), jnp.float32)
-        for level in reversed(range(levels)):
-            u, v, h = field[level, s], field[levels + level, s], field[2 * levels + level, s]
-            geo = total + 0.5 * h
-            total = total + h
-            zonal = (0.25 * time_step) * (h + east(h)) * (u + east(u))
-            merid = jnp.where(top, 0.0, (h + pltpu.roll(h, 1, 0)) * (v + pltpu.roll(v, 1, 0)) * edge)
-            result[2 * levels + level, s] = h - ((zonal - west(zonal)) + (up(merid, 0.0) - merid))
-            result[level, s] = u - (0.5 * time_step) * (east(geo) - west(geo)) + sin_center * v
-            result[levels + level, s] = v - cos_center * (up(geo, 0.0) - down(geo, 0.0)) - sin_center * u
-        return carry
-
-    lax.fori_loop(0, RADIX, stencil, 0)
+    def inside(first, last):
+        sin_center, cos_center, edge = trig[0], trig[1], trig[2]
+
+        def one_segment(s, carry):
+            total = jnp.zeros((rows, WIDE), jnp.float32)
+            for level in reversed(range(levels)):
+                u, v, h = field[level, s], field[levels + level, s], field[2 * levels + level, s]
+                geo = total + 0.5 * h
+                total = total + h
+                zonal = (0.25 * time_step) * (h + east(h)) * (u + east(u))
+                merid = jnp.where(top, 0.0, (h + pltpu.roll(h, 1, 0)) * (v + pltpu.roll(v, 1, 0)) * edge)
+                result[2 * levels + level, s] = h - ((zonal - west(zonal)) + (up(merid, 0.0) - merid))
+                result[level, s] = u - (0.5 * time_step) * (east(geo) - west(geo)) + sin_center * v
+                result[levels + level, s] = v - cos_center * (up(geo, 0.0) - down(geo, 0.0)) - sin_center * u
+            return carry
+
+        lax.fori_loop(first, last, one_segment, 0)
 
     def write_rows(target, source, parts):
         for p in parts:
@@ -539,16 +515,43 @@
 
         lax.fori_loop(0, levels, unit, 0)
 
-    write_units(0, range(4))
     stores = [
         pltpu.make_async_copy(out.at[pl.ds(0, levels)], part_winds.at[0], store_sem.at[0]),
         pltpu.make_async_copy(out.at[pl.ds(levels, levels)], part_winds.at[1], store_sem.at[1]),
         pltpu.make_async_copy(out.at[pl.ds(2 * levels, levels)], new_thick, store_sem.at[2]),
         pltpu.make_async_copy(out_delta, delta, store_sem.at[3]),
     ]
-    stores[0].start()
-    write_units(levels, (1, 2))
-    write_units(2 * levels, (1, 2))
+
+    def write_first():
+        write_units(0, range(4))
+        stores[0].start()
+
+    def write_middle():
+        write_units(levels, (1, 2))
+        write_units(2 * levels, (1, 2))
+
+    def rest_of_loads():
+        for load in loads[2:]:
+            load.wait()
+
+    def run(*stages):
+        for stage in stages:
+            stage()
+
+    half_way = RADIX // 2
+    some = lambda stage, *args: functools.partial(stage, *args)
+
+    @pl.when(early)
+    def _():
+        run(rest_of_loads, limits, forward_thick, forward_winds, some(products, range(6)), inverse)
+        run(enter, first_step, neighbours, some(inside, 0, half_way), row_first, second_step)
+        run(some(inside, half_way, RADIX), row_second, share, write_first, write_middle)
+
+    @pl.when(jnp.logical_not(early))
+    def _():
+        run(enter, limits, forward_thick, first_step, rest_of_loads, forward_winds, some(products, range(3)))
+        run(second_step, some(products, range(3, 6)), share, inverse, neighbours)
+        run(some(inside, 0, half_way), row_first, some(inside, half_way, RADIX), write_first, row_second, write_middle)
 
     for i, c in enumerate(pieces):
         shares[i].wait()
@@ -562,6 +565,9 @@
     def _():
         row_up_first.wait_recv()
 
+    sin_center, cos_center, edge = trig[0], trig[1], trig[2]
+    last_index = (lat * rows + rows + jnp.zeros((8, WIDE), jnp.int32)).astype(jnp.float32)
+    last_edge = (0.25 * time_step) * jnp.sin(last_index * (math.pi / lat_total))
     minus_cut = from_minus[:, full - WIDE :][:, WIDE - 1 :]
     plus_cut = from_plus[:, full - WIDE :][:, WIDE - 1 :]
     cut2[pl.ds(rows, 8), :] = jnp.broadcast_to(minus_cut, (8, WIDE))
@@ -646,7 +652,7 @@
     bf16 = lambda *dims: pltpu.VMEM(dims, jnp.bfloat16)
     hbm = pl.BlockSpec(memory_space=pl.ANY)
     return pl.pallas_call(
-        functools.partial(step_kernel, shape["lat"], shape["lev"], 2 if shape["lat"] == 64 else 1),
+        functools.partial(step_kernel, shape["lat"], shape["lev"], 1),
         out_shape=(
             jax.ShapeDtypeStruct(winds.shape, jnp.float32),
             jax.ShapeDtypeStruct(thick.shape, jnp.float32),
@@ -673,6 +679,7 @@
             f32(more, WIDE),
             f32(3 * levels, rows, lon),
             f32(2, rows, lon),
+            f32(3, rows, WIDE),
             f32(8, full),
             f32(8, full),
             f32(8, full),
@@ -700,12 +707,57 @@
     )(thick, winds, cutoff, jnp.asarray(wave), jnp.asarray(high), jnp.asarray(low))
 
 
+def last_kernel(part_winds, part_thick, delta, new_winds, new_thick, w, t, d, in_sem, out_sem):
+    levels = t.shape[0]
+    pieces = [(part_winds.at[f, level], w.at[f, level], new_winds.at[f, level]) for f in range(2) for level in range(levels)]
+    pieces.append((part_thick, t, new_thick))
+    grads = [pltpu.make_async_copy(delta.at[f], d.at[f], in_sem.at[len(pieces) + f]) for f in range(2)]
+    loads = [pltpu.make_async_copy(source, held, in_sem.at[i]) for i, (source, held, _) in enumerate(pieces)]
+    stores = [pltpu.make_async_copy(held, target, out_sem.at[i]) for i, (_, held, target) in enumerate(pieces)]
+    for f in range(2):
+        grads[f].start()
+        for load in loads[f * levels : (f + 1) * levels]:
+            load.start()
+    loads[-1].start()
+    for f in range(2):
+        grads[f].wait()
+        for level in range(levels):
+            at = f * levels + level
+            loads[at].wait()
+            w[f, level] = w[f, level] + d[f]
+            stores[at].start()
+    loads[-1].wait()
+    stores[-1].start()
+    for store in stores:
+        store.wait()
+
+
+def last(part_winds, part_thick, delta):
+    hbm = pl.BlockSpec(memory_space=pl.ANY)
+    count = 2 * part_thick.shape[0] + 1
+    return pl.pallas_call(
+        last_kernel,
+        out_shape=(
+            jax.ShapeDtypeStruct(part_winds.shape, jnp.float32),
+            jax.ShapeDtypeStruct(part_thick.shape, jnp.float32),
+        ),
+        in_specs=[hbm, hbm, hbm],
+        out_specs=(hbm, hbm),
+        scratch_shapes=[
+            pltpu.VMEM(part_winds.shape, jnp.float32),
+            pltpu.VMEM(part_thick.shape, jnp.float32),
+            pltpu.VMEM(delta.shape, jnp.float32),
+            pltpu.SemaphoreType.DMA((count + 2,)),
+            pltpu.SemaphoreType.DMA((count,)),
+        ],
+    )(part_winds, part_thick, delta)
+
+
 def solution(mesh):
     shape = dict(mesh.shape)
 
     def per_device(winds, thickness, cutoff):
-        part_winds, new_thick, delta = step(shape, winds, thickness, cutoff)
-        return part_winds + delta[:, None], new_thick
+        return last(*step(shape, winds, thickness, cutoff))
 
     return jax.shard_map(
         per_device,

time: 33.9 us -> 31.1 us (0.917)
  other arithmetic: 2.83 us -> 0 us
  Pallas kernels: 29.3 us -> 30.2 us
  local copies, waits for them, and re-layouts: 0.88 us -> 0 us
    pallas_call x0 -> x1, Pallas kernels: none -> 2.9 us  [last(): pl.pallas_call(last_kernel, out_shape=(jax.ShapeDtypeStruct(part_winds.sh...]
    add x1 -> x0, other arithmetic: 2.83 us -> none  [per_device(): return (part_winds + delta[:, None], new_thick)]
    pallas_call x1, Pallas kernels: 29.3 us -> 27.3 us  [step(): pl.pallas_call(functools.partial(step_kernel, shape['lat'], shape['lev'],...]
    unnamed x3 -> x0, local copies, waits for them, and re-layouts: 0.88 us -> none
where the time goes in v3:
time: 31.1 us; the launch traced here: 30.9 us
  Pallas kernels  30.2 us (97%)
  between operations  0.64 us (2%)
    pallas_call x1, Pallas kernels, step(): pl.pallas_call(functools.partial(step_kernel, shape['lat'], shape['lev'],...  27.3 us
    pallas_call x1, Pallas kernels, last(): pl.pallas_call(last_kernel, out_shape=(jax.ShapeDtypeStruct(part_winds.sh...  2.9 us

profile of v3, /device:TPU:50, one launch (start us, length us, event | category | flops | bytes accessed | tf_op | source)
XLA Modules:
  0.0 30.9 jit_solution(11072537624656262855)
XLA Ops:
  0.6 27.3 %shard_map.77 = (f32[2,4,32,1440]{3,2,1,0:T(8,128)}, f32[4,32,1440]{2,1,0:T(8,128)}, f32[2,32,1440]{2,1,0:T(8,128)}) custom-call(f32[4,32,1440]{2,1,0:T(8,128)} %thick.1, f32[2,4,32,1440]{3,2,1,0:T(8,128)} %winds.1, s32[32]{0:T(128)} %cutoff.1, f32[1,1536]{1,0:T(1,128)} %constant.6.clone.wave, bf16[6,256,256]{2,1,0:T(8,128)(2,1)} %constant.7.clone.table_high, ...), custom_call_target="tpu_custom_call" | custom-call | tf_op jit(solution)/shard_map/pallas_call | solution.py:654
  28.0 2.9 %shard_map.78 = (f32[2,4,32,1440]{3,2,1,0:T(8,128)}, f32[4,32,1440]{2,1,0:T(8,128)}) custom-call(f32[2,4,32,1440]{3,2,1,0:T(8,128)} %get-tuple-element.5.part_winds, f32[4,32,1440]{2,1,0:T(8,128)} %get-tuple-element.6.part_thick, f32[2,32,1440]{2,1,0:T(8,128)} %get-tuple-element.7.delta), custom_call_target="tpu_custom_call" | custom-call | tf_op jit(solution)/shard_map/pallas_call | solution.py:738

commit v4 on v3

--- a/solution.py
+++ b/solution.py
@@ -163,13 +163,15 @@
     early_count,
     thick,
     winds,
-    cutoff,
-    wave,
+    cutoff_in,
+    wave_in,
     table_high,
     table_low,
     part_winds,
     new_thick,
     delta,
+    cutoff,
+    wave,
     h_in,
     w_in,
     f_high,
@@ -224,6 +226,7 @@
     has_minus, has_plus = lat > 0, lat < lat_count - 1
     lat_minus, lat_plus = jnp.maximum(lat - 1, 0), jnp.minimum(lat + 1, lat_count - 1)
     early = lat % 8 < early_count
+    after_early = lat % 8 == early_count
 
     barrier = pltpu.get_barrier_semaphore()
     for device in ((lat, partner), (lat, x_up), (lat, x_down)):
@@ -243,13 +246,15 @@
             (
                 (thick, h_in),
                 (winds.at[1], w_in.at[1]),
+                (cutoff_in, cutoff),
+                (wave_in, wave),
                 (table_high, f_high),
                 (table_low, f_low),
                 (winds.at[0], w_in.at[0]),
             )
         )
     ]
-    for load in loads:
+    for load in loads[:3]:
         load.start()
 
     def remote(source, target, at, device):
@@ -308,12 +313,15 @@
         lax.fori_loop(0, fields, unit, 0)
 
     loads[0].wait()
+    for load in loads[3:]:
+        load.start()
     total = h_in[0]
     for level in range(1, levels):
         total = total + h_in[level]
     column[:, pl.ds(full - WIDE, WIDE)] = jnp.zeros((rows, WIDE), jnp.float32)
     column[:, pl.ds(0, lon)] = total
     loads[1].wait()
+    loads[2].wait()
     row8 = lax.broadcasted_iota(jnp.int32, (8, lon), 0)
     for pack, row in ((send_minus, 0), (send_plus, rows - 1)):
         value = jnp.zeros((8, lon), jnp.float32)
@@ -327,21 +335,24 @@
     mine, theirs = pl.multiple_of(core * part, part), pl.multiple_of((1 - core) * part, part)
     upper = jnp.where(core == 0, 0.0, 1.0)
     lower = 1.0 - upper
-    pieces = [pl.ds(8 * i, 8) for i in range(2)]
-    places = [pl.ds(pl.multiple_of(mine + 8 * i, 8), 8) for i in range(2)]
+    chunks = [(8 * r, full // 2 * c) for r in range(part // 8) for c in range(2)]
+    pieces = [(pl.ds(r, 8), pl.ds(c, full // 2)) for r, c in chunks]
+    places = [(pl.ds(pl.multiple_of(mine + r, 8), 8), pl.ds(c, full // 2)) for r, c in chunks]
+    others = [(pl.ds(pl.multiple_of(theirs + r, 8), 8), pl.ds(c, full // 2)) for r, c in chunks]
+    count = len(pieces)
     to_pair = remote(column.at[pl.ds(theirs, part), :], pair, 0, (lat, partner))
     to_minus = remote(send_minus, from_plus, 1, (lat_minus, lev))
     to_plus = remote(send_plus, from_minus, 2, (lat_plus, lev))
-    down_first = [remote(sums.at[c, :], from_upper.at[c, :], 3 + i, (lat, x_down)) for i, c in enumerate(pieces)]
-    down_later = [remote(relay.at[c, :], from_upper.at[c, :], 3 + i, (lat, x_down)) for i, c in enumerate(pieces)]
-    up_first = [remote(sums.at[c, :], from_lower.at[c, :], 5 + i, (lat, x_up)) for i, c in enumerate(pieces)]
-    up_later = [remote(from_lower.at[c, :], from_lower.at[c, :], 5 + i, (lat, x_up)) for i, c in enumerate(pieces)]
-    row_pairing = remote(row_column, row_pair, 7, (lat, partner))
-    row_down_first = remote(row_sums, row_upper, 8, (lat, x_down))
-    row_down_later = remote(row_relay, row_upper, 8, (lat, x_down))
-    row_up_first = remote(row_sums, row_lower, 9, (lat, x_up))
-    row_up_later = remote(row_lower, row_lower, 9, (lat, x_up))
-    shares = [remote(column.at[p, :], shared.at[c, :], 10 + i, (lat, partner)) for i, (p, c) in enumerate(zip(places, pieces))]
+    down_first = [remote(sums.at[*c], from_upper.at[*c], 3 + i, (lat, x_down)) for i, c in enumerate(pieces)]
+    down_later = [remote(relay.at[*c], from_upper.at[*c], 3 + i, (lat, x_down)) for i, c in enumerate(pieces)]
+    up_first = [remote(sums.at[*c], from_lower.at[*c], 3 + count + i, (lat, x_up)) for i, c in enumerate(pieces)]
+    up_later = [remote(from_lower.at[*c], from_lower.at[*c], 3 + count + i, (lat, x_up)) for i, c in enumerate(pieces)]
+    row_pairing = remote(row_column, row_pair, 3 + 3 * count, (lat, partner))
+    row_down_first = remote(row_sums, row_upper, 4 + 3 * count, (lat, x_down))
+    row_down_later = remote(row_relay, row_upper, 4 + 3 * count, (lat, x_down))
+    row_up_first = remote(row_sums, row_lower, 5 + 3 * count, (lat, x_up))
+    row_up_later = remote(row_lower, row_lower, 5 + 3 * count, (lat, x_up))
+    shares = [remote(column.at[*p], shared.at[*c], 3 + 2 * count + i, (lat, partner)) for i, (p, c) in enumerate(zip(places, pieces))]
 
     def enter():
         pl.semaphore_wait(barrier, 3 + one(has_minus) + one(has_plus))
@@ -358,7 +369,7 @@
     def first_step():
         to_pair.wait()
         sums[...] = column[pl.ds(mine, part), :] + pair[...]
-        for i in range(2):
+        for i in range(count):
             @pl.when(x >= 2)
             def _():
                 down_first[i].start()
@@ -385,7 +396,7 @@
 
             @pl.when(x == 1)
             def _():
-                relay[c, :] = sums[c, :] + from_upper[c, :]
+                relay[*c] = sums[*c] + from_upper[*c]
                 down_later[i].start()
 
             @pl.when(x == 0)
@@ -403,9 +414,9 @@
             def _():
                 up_first[i].wait_recv()
 
-            above = from_upper[c, :] + from_lower[c, :]
-            below[p, :] = above + lower * pair[c, :]
-            column[p, :] = above + upper * column[p, :]
+            above = from_upper[*c] + from_lower[*c]
+            below[*p] = above + lower * pair[*c]
+            column[*p] = above + upper * column[*p]
             shares[i].start()
 
     def neighbours():
@@ -531,7 +542,7 @@
         write_units(2 * levels, (1, 2))
 
     def rest_of_loads():
-        for load in loads[2:]:
+        for load in loads[3:]:
             load.wait()
 
     def run(*stages):
@@ -544,18 +555,24 @@
     @pl.when(early)
     def _():
         run(rest_of_loads, limits, forward_thick, forward_winds, some(products, range(6)), inverse)
-        run(enter, first_step, neighbours, some(inside, 0, half_way), row_first, second_step)
-        run(some(inside, half_way, RADIX), row_second, share, write_first, write_middle)
-
-    @pl.when(jnp.logical_not(early))
+        run(some(inside, 0, RADIX), write_first, write_middle)
+        run(enter, first_step, neighbours, row_first, second_step, row_second, share)
+
+    @pl.when(after_early)
     def _():
         run(enter, limits, forward_thick, first_step, rest_of_loads, forward_winds, some(products, range(3)))
-        run(second_step, some(products, range(3, 6)), share, inverse, neighbours)
-        run(some(inside, 0, half_way), row_first, some(inside, half_way, RADIX), write_first, row_second, write_middle)
+        run(second_step, some(products, range(3, 6)), share, inverse, some(inside, 0, half_way), neighbours)
+        run(some(inside, half_way, RADIX), row_first, write_first, row_second, write_middle)
+
+    @pl.when(jnp.logical_not(early | after_early))
+    def _():
+        run(enter, limits, forward_thick, first_step, rest_of_loads, forward_winds, neighbours)
+        run(some(products, range(3)), row_first, second_step, some(products, range(3, 6)), row_second)
+        run(inverse, share, some(inside, 0, RADIX), write_first, write_middle)
 
     for i, c in enumerate(pieces):
         shares[i].wait()
-        below[pl.ds(pl.multiple_of(theirs + 8 * i, 8), 8), :] = shared[c, :]
+        below[*others[i]] = shared[*c]
 
     @pl.when(x == 0)
     def _():
@@ -650,7 +667,8 @@
     more = rows + 32
     f32 = lambda *dims: pltpu.VMEM(dims, jnp.float32)
     bf16 = lambda *dims: pltpu.VMEM(dims, jnp.bfloat16)
-    hbm = pl.BlockSpec(memory_space=pl.ANY)
+    hbm = pl.BlockSpec(memory_space=pltpu.HBM)
+    free = pl.BlockSpec(memory_space=pl.ANY)
     return pl.pallas_call(
         functools.partial(step_kernel, shape["lat"], shape["lev"], 1),
         out_shape=(
@@ -658,9 +676,11 @@
             jax.ShapeDtypeStruct(thick.shape, jnp.float32),
             jax.ShapeDtypeStruct((2, rows, lon), jnp.float32),
         ),
-        in_specs=[hbm, hbm, pl.BlockSpec(memory_space=pltpu.SMEM), pl.BlockSpec(memory_space=pltpu.VMEM), hbm, hbm],
-        out_specs=(hbm, hbm, hbm),
+        in_specs=[hbm] * 6,
+        out_specs=(free, free, free),
         scratch_shapes=[
+            pltpu.SMEM((rows,), jnp.int32),
+            f32(1, RADIX * WIDE),
             f32(levels, rows, lon),
             f32(2, levels, rows, lon),
             bf16(*high.shape),
@@ -698,58 +718,45 @@
             f32(2, 1, full),
             f32(2, 1, full),
             f32(2, 1, full),
-            pltpu.SemaphoreType.DMA((5,)),
+            pltpu.SemaphoreType.DMA((7,)),
             pltpu.SemaphoreType.DMA((4,)),
-            pltpu.SemaphoreType.DMA((12,)),
-            pltpu.SemaphoreType.DMA((12,)),
+            pltpu.SemaphoreType.DMA((18,)),
+            pltpu.SemaphoreType.DMA((18,)),
         ],
-        compiler_params=pltpu.CompilerParams(collective_id=0, has_side_effects=True, vmem_limit_bytes=56 << 20),
-    )(thick, winds, cutoff, jnp.asarray(wave), jnp.asarray(high), jnp.asarray(low))
-
-
-def last_kernel(part_winds, part_thick, delta, new_winds, new_thick, w, t, d, in_sem, out_sem):
-    levels = t.shape[0]
-    pieces = [(part_winds.at[f, level], w.at[f, level], new_winds.at[f, level]) for f in range(2) for level in range(levels)]
-    pieces.append((part_thick, t, new_thick))
-    grads = [pltpu.make_async_copy(delta.at[f], d.at[f], in_sem.at[len(pieces) + f]) for f in range(2)]
-    loads = [pltpu.make_async_copy(source, held, in_sem.at[i]) for i, (source, held, _) in enumerate(pieces)]
-    stores = [pltpu.make_async_copy(held, target, out_sem.at[i]) for i, (_, held, target) in enumerate(pieces)]
+        compiler_params=pltpu.CompilerParams(collective_id=0, has_side_effects=True, vmem_limit_bytes=24 << 20),
+    )(*[pltpu.with_memory_space_constraint(v, pltpu.HBM) for v in (thick, winds, cutoff, jnp.asarray(wave), jnp.asarray(high), jnp.asarray(low))])
+
+
+def last_kernel(part_winds, part_thick, delta, new_winds, new_thick, w, sem):
+    levels = part_thick.shape[0]
+    stores = [pltpu.make_async_copy(part_thick, new_thick, sem.at[2 * levels])]
+    stores[0].start()
     for f in range(2):
-        grads[f].start()
-        for load in loads[f * levels : (f + 1) * levels]:
-            load.start()
-    loads[-1].start()
-    for f in range(2):
-        grads[f].wait()
         for level in range(levels):
-            at = f * levels + level
-            loads[at].wait()
-            w[f, level] = w[f, level] + d[f]
-            stores[at].start()
-    loads[-1].wait()
-    stores[-1].start()
+            w[f, level] = part_winds[f, level] + delta[f]
+            store = pltpu.make_async_copy(w.at[f, level], new_winds.at[f, level], sem.at[f * levels + level])
+            store.start()
+            stores.append(store)
     for store in stores:
         store.wait()
 
 
 def last(part_winds, part_thick, delta):
-    hbm = pl.BlockSpec(memory_space=pl.ANY)
-    count = 2 * part_thick.shape[0] + 1
+    hbm = pl.BlockSpec(memory_space=pltpu.HBM)
+    vmem = pl.BlockSpec(memory_space=pltpu.VMEM)
     return pl.pallas_call(
         last_kernel,
         out_shape=(
             jax.ShapeDtypeStruct(part_winds.shape, jnp.float32),
             jax.ShapeDtypeStruct(part_thick.shape, jnp.float32),
         ),
-        in_specs=[hbm, hbm, hbm],
+        in_specs=[vmem, vmem, vmem],
         out_specs=(hbm, hbm),
         scratch_shapes=[
             pltpu.VMEM(part_winds.shape, jnp.float32),
-            pltpu.VMEM(part_thick.shape, jnp.float32),
-            pltpu.VMEM(delta.shape, jnp.float32),
-            pltpu.SemaphoreType.DMA((count + 2,)),
-            pltpu.SemaphoreType.DMA((count,)),
+            pltpu.SemaphoreType.DMA((2 * part_thick.shape[0] + 1,)),
         ],
+        compiler_params=pltpu.CompilerParams(vmem_limit_bytes=8 << 20),
     )(part_winds, part_thick, delta)
 
 

time: 31.1 us -> 31.5 us (1.013)
  the two profiles are of different devices: /device:TPU:50 before, /device:TPU:3 now
where the time goes in v4:
time: 31.5 us; the launch traced here: 31.3 us
  Pallas kernels  30.7 us (97%)
  between operations  0.64 us (2%)
    pallas_call x1, Pallas kernels, step(): pl.pallas_call(functools.partial(step_kernel, shape['lat'], shape['lev'],...  29.2 us
    pallas_call x1, Pallas kernels, last(): pl.pallas_call(last_kernel, out_shape=(jax.ShapeDtypeStruct(part_winds.sh...  1.47 us

profile of v4, /device:TPU:3, one launch (start us, length us, event | category | flops | bytes accessed | tf_op | source)
XLA Modules:
  0.0 31.3 jit_solution(4503642317437839898)
XLA Ops:
  0.6 29.2 %shard_map.77 = (f32[2,4,32,1440]{3,2,1,0:T(8,128)S(1)}, f32[4,32,1440]{2,1,0:T(8,128)S(1)}, f32[2,32,1440]{2,1,0:T(8,128)S(1)}) custom-call(f32[4,32,1440]{2,1,0:T(8,128)} %thick.1, f32[2,4,32,1440]{3,2,1,0:T(8,128)} %winds.1, s32[32]{0:T(128)} %cutoff_in.1, f32[1,1536]{1,0:T(1,128)} %constant.6.clone.wave_in, ...), custom_call_target="tpu_custom_call" | custom-call | tf_op jit(solution)/shard_map/pallas_call | solution.py:672
  29.9 1.5 %shard_map.78 = (f32[2,4,32,1440]{3,2,1,0:T(8,128)}, f32[4,32,1440]{2,1,0:T(8,128)}) custom-call(f32[2,4,32,1440]{3,2,1,0:T(8,128)S(1)} %get-tuple-element.5.part_winds, f32[4,32,1440]{2,1,0:T(8,128)S(1)} %get-tuple-element.6.part_thick, f32[2,32,1440]{2,1,0:T(8,128)S(1)} %get-tuple-element.7.delta), custom_call_target="tpu_custom_call" | custom-call | tf_op jit(solution)/shard_map/pallas_call | solution.py:747

commit v5 on v4

--- a/solution.py
+++ b/solution.py
@@ -160,7 +160,6 @@
 def step_kernel(
     lat_count,
     lev_count,
-    early_count,
     thick,
     winds,
     cutoff_in,
@@ -206,9 +205,8 @@
     row_column,
     row_pair,
     row_sums,
-    row_upper,
-    row_lower,
-    row_relay,
+    row_slots,
+    send_row,
     load_sem,
     store_sem,
     send_sem,
@@ -222,14 +220,15 @@
     x, core = lev // 2, lev % 2
     chips = lev_count // 2
     partner = x * 2 + (1 - core)
+    chip_at = lambda other: ((other + chips) % chips) * 2 + core
     x_up, x_down = ((x + 1) % chips) * 2 + core, ((x + chips - 1) % chips) * 2 + core
     has_minus, has_plus = lat > 0, lat < lat_count - 1
     lat_minus, lat_plus = jnp.maximum(lat - 1, 0), jnp.minimum(lat + 1, lat_count - 1)
-    early = lat % 8 < early_count
-    after_early = lat % 8 == early_count
+    early = (lat % 8 == 0) & (lat > 0)
+    after_early = lat % 8 == 1
 
     barrier = pltpu.get_barrier_semaphore()
-    for device in ((lat, partner), (lat, x_up), (lat, x_down)):
+    for device in ((lat, partner), (lat, x_up), (lat, x_down), (lat, chip_at(x + 2))):
         pl.semaphore_signal(barrier, inc=1, device_id=device, device_id_type=MESH)
 
     @pl.when(has_minus)
@@ -320,6 +319,8 @@
         total = total + h_in[level]
     column[:, pl.ds(full - WIDE, WIDE)] = jnp.zeros((rows, WIDE), jnp.float32)
     column[:, pl.ds(0, lon)] = total
+    send_row[0] = column[0:1, :]
+    send_row[1] = column[rows - 1 : rows, :]
     loads[1].wait()
     loads[2].wait()
     row8 = lax.broadcasted_iota(jnp.int32, (8, lon), 0)
@@ -348,14 +349,21 @@
     up_first = [remote(sums.at[*c], from_lower.at[*c], 3 + count + i, (lat, x_up)) for i, c in enumerate(pieces)]
     up_later = [remote(from_lower.at[*c], from_lower.at[*c], 3 + count + i, (lat, x_up)) for i, c in enumerate(pieces)]
     row_pairing = remote(row_column, row_pair, 3 + 3 * count, (lat, partner))
-    row_down_first = remote(row_sums, row_upper, 4 + 3 * count, (lat, x_down))
-    row_down_later = remote(row_relay, row_upper, 4 + 3 * count, (lat, x_down))
-    row_up_first = remote(row_sums, row_lower, 5 + 3 * count, (lat, x_up))
-    row_up_later = remote(row_lower, row_lower, 5 + 3 * count, (lat, x_up))
+    row_minus = remote(send_row.at[0], row_column.at[1], 4 + 3 * count, (lat_minus, lev))
+    row_plus = remote(send_row.at[1], row_column.at[0], 5 + 3 * count, (lat_plus, lev))
+    row_links = [remote(row_sums, row_slots.at[j - 1], 5 + 3 * count + j, (lat, chip_at(x - j))) for j in range(1, 4)]
     shares = [remote(column.at[*p], shared.at[*c], 3 + 2 * count + i, (lat, partner)) for i, (p, c) in enumerate(zip(places, pieces))]
 
     def enter():
-        pl.semaphore_wait(barrier, 3 + one(has_minus) + one(has_plus))
+        pl.semaphore_wait(barrier, 4 + one(has_minus) + one(has_plus))
+        @pl.when(has_minus)
+        def _():
+            row_minus.start()
+
+        @pl.when(has_plus)
+        def _():
+            row_plus.start()
+
         to_pair.start()
 
         @pl.when(has_minus)
@@ -381,15 +389,14 @@
         @pl.when(x == chips - 1)
         def _():
             from_upper[...] = jnp.zeros_like(from_upper)
-            row_upper[...] = jnp.zeros_like(row_upper)
 
         @pl.when(x >= chips - 2)
         def _():
             from_lower[...] = jnp.zeros_like(from_lower)
-            row_lower[...] = jnp.zeros_like(row_lower)
-
-    def second_step():
-        for i, c in enumerate(pieces):
+
+    def second_step(which):
+        for i in which:
+            c = pieces[i]
             @pl.when((x == 1) | (x == 2))
             def _():
                 down_first[i].wait_recv()
@@ -419,6 +426,27 @@
             column[*p] = above + upper * column[*p]
             shares[i].start()
 
+    def rows_in():
+        @pl.when(has_minus)
+        def _():
+            row_minus.wait_send()
+            row_plus.wait_recv()
+
+        @pl.when(jnp.logical_not(has_minus))
+        def _():
+            row_column[0] = jnp.zeros((1, full), jnp.float32)
+
+        @pl.when(has_plus)
+        def _():
+            row_plus.wait_send()
+            row_minus.wait_recv()
+
+        @pl.when(jnp.logical_not(has_plus))
+        def _():
+            row_column[1] = jnp.zeros((1, full), jnp.float32)
+
+        row_pairing.start()
+
     def neighbours():
         @pl.when(has_minus)
         def _():
@@ -438,39 +466,18 @@
         def _():
             from_plus[...] = jnp.zeros_like(from_plus)
 
-        for at, source in enumerate((from_minus, from_plus)):
-            outside = source[0:1, :]
-            for level in range(1, levels):
-                outside = outside + source[level : level + 1, :]
-            row_column[at] = outside
-        row_pairing.start()
 
     def row_first():
         row_pairing.wait()
         row_sums[...] = row_column[...] + row_pair[...]
-
-        @pl.when(x >= 2)
-        def _():
-            row_down_first.start()
-
-        @pl.when(x == 3)
-        def _():
-            row_up_first.start()
-
-    def row_second():
-        @pl.when((x == 1) | (x == 2))
-        def _():
-            row_down_first.wait_recv()
-
-        @pl.when(x == 1)
-        def _():
-            row_relay[...] = row_sums[...] + row_upper[...]
-            row_down_later.start()
-
-        @pl.when(x == 0)
-        def _():
-            row_up_first.wait_recv()
-            row_up_later.start()
+        for j, link in enumerate(row_links, 1):
+            @pl.when(x >= j)
+            def _():
+                link.start()
+
+            @pl.when(x + j >= chips)
+            def _():
+                row_slots[j - 1] = jnp.zeros((2, 1, full), jnp.float32)
 
     row_index = (lat * rows + row32).astype(jnp.float32)
     lat_total = lat_count * rows
@@ -549,38 +556,35 @@
         for stage in stages:
             stage()
 
-    half_way = RADIX // 2
     some = lambda stage, *args: functools.partial(stage, *args)
 
     @pl.when(early)
     def _():
         run(rest_of_loads, limits, forward_thick, forward_winds, some(products, range(6)), inverse)
         run(some(inside, 0, RADIX), write_first, write_middle)
-        run(enter, first_step, neighbours, row_first, second_step, row_second, share)
+        run(enter, first_step, rows_in, some(second_step, range(count // 2)), row_first)
+        run(some(second_step, range(count // 2, count)), share, neighbours)
 
     @pl.when(after_early)
     def _():
         run(enter, limits, forward_thick, first_step, rest_of_loads, forward_winds, some(products, range(3)))
-        run(second_step, some(products, range(3, 6)), share, inverse, some(inside, 0, half_way), neighbours)
-        run(some(inside, half_way, RADIX), row_first, write_first, row_second, write_middle)
+        run(some(second_step, range(count)), some(products, range(3, 6)), share, inverse, some(inside, 0, RADIX))
+        run(write_first, rows_in, write_middle, row_first, neighbours)
 
     @pl.when(jnp.logical_not(early | after_early))
     def _():
-        run(enter, limits, forward_thick, first_step, rest_of_loads, forward_winds, neighbours)
-        run(some(products, range(3)), row_first, second_step, some(products, range(3, 6)), row_second)
-        run(inverse, share, some(inside, 0, RADIX), write_first, write_middle)
+        run(enter, limits, forward_thick, first_step, rest_of_loads, forward_winds, some(products, range(3)))
+        run(some(second_step, range(count)), rows_in, some(products, range(3, 6)), row_first, inverse, share)
+        run(some(inside, 0, RADIX), write_first, write_middle, neighbours)
 
     for i, c in enumerate(pieces):
         shares[i].wait()
         below[*others[i]] = shared[*c]
 
-    @pl.when(x == 0)
-    def _():
-        row_down_first.wait_recv()
-
-    @pl.when(x == 1)
-    def _():
-        row_up_first.wait_recv()
+    for j, link in enumerate(row_links, 1):
+        @pl.when(x + j < chips)
+        def _():
+            link.wait_recv()
 
     sin_center, cos_center, edge = trig[0], trig[1], trig[2]
     last_index = (lat * rows + rows + jnp.zeros((8, WIDE), jnp.int32)).astype(jnp.float32)
@@ -595,7 +599,7 @@
         forward_rows(tiles_of(lambda c: below[pl.ds(half * 16, 16), c]), y2_high, y2_low, half * 16)
     forward_rows(tiles_of(lambda c: jnp.concatenate([from_minus[:, c], from_plus[:, c]], axis=0)), y2_high, y2_low, rows)
     for at in range(2):
-        row_column[at] = row_upper[at] + row_lower[at] + lower * row_pair[at]
+        row_column[at] = row_slots[0, at] + row_slots[1, at] + row_slots[2, at] + lower * row_pair[at]
 
     def edge_tile(c):
         return jnp.where(row16 == 0, row_column[0, :, c], jnp.where(row16 == 1, row_column[1, :, c], 0.0))
@@ -646,13 +650,16 @@
     def _():
         for link in down_first:
             link.wait_send()
-        row_down_first.wait_send()
 
     @pl.when((x == 0) | (x == 3))
     def _():
         for link in up_first:
             link.wait_send()
-        row_up_first.wait_send()
+
+    for j, link in enumerate(row_links, 1):
+        @pl.when(x >= j)
+        def _():
+            link.wait_send()
 
     for store in stores:
         store.wait()
@@ -670,7 +677,7 @@
     hbm = pl.BlockSpec(memory_space=pltpu.HBM)
     free = pl.BlockSpec(memory_space=pl.ANY)
     return pl.pallas_call(
-        functools.partial(step_kernel, shape["lat"], shape["lev"], 1),
+        functools.partial(step_kernel, shape["lat"], shape["lev"]),
         out_shape=(
             jax.ShapeDtypeStruct(winds.shape, jnp.float32),
             jax.ShapeDtypeStruct(thick.shape, jnp.float32),
@@ -715,13 +722,12 @@
             f32(2, 1, full),
             f32(2, 1, full),
             f32(2, 1, full),
-            f32(2, 1, full),
-            f32(2, 1, full),
+            f32(3, 2, 1, full),
             f32(2, 1, full),
             pltpu.SemaphoreType.DMA((7,)),
             pltpu.SemaphoreType.DMA((4,)),
-            pltpu.SemaphoreType.DMA((18,)),
-            pltpu.SemaphoreType.DMA((18,)),
+            pltpu.SemaphoreType.DMA((21,)),
+            pltpu.SemaphoreType.DMA((21,)),
         ],
         compiler_params=pltpu.CompilerParams(collective_id=0, has_side_effects=True, vmem_limit_bytes=24 << 20),
     )(*[pltpu.with_memory_space_constraint(v, pltpu.HBM) for v in (thick, winds, cutoff, jnp.asarray(wave), jnp.asarray(high), jnp.asarray(low))])

time: 31.5 us -> 29.2 us (0.927)
  the two profiles are of different devices: /device:TPU:3 before, /device:TPU:11 now
where the time goes in v5:
time: 29.2 us; the launch traced here: 29 us
  Pallas kernels  28.4 us (97%)
  between operations  0.64 us (2%)
    pallas_call x1, Pallas kernels, step(): pl.pallas_call(functools.partial(step_kernel, shape['lat'], shape['lev'])...  26.9 us
    pallas_call x1, Pallas kernels, last(): pl.pallas_call(last_kernel, out_shape=(jax.ShapeDtypeStruct(part_winds.sh...  1.47 us

profile of v5, /device:TPU:11, one launch (start us, length us, event | category | flops | bytes accessed | tf_op | source)
XLA Modules:
  0.0 29.0 jit_solution(7330879568551055118)
XLA Ops:
  0.6 26.9 %shard_map.77 = (f32[2,4,32,1440]{3,2,1,0:T(8,128)S(1)}, f32[4,32,1440]{2,1,0:T(8,128)S(1)}, f32[2,32,1440]{2,1,0:T(8,128)S(1)}) custom-call(f32[4,32,1440]{2,1,0:T(8,128)} %thick.1, f32[2,4,32,1440]{3,2,1,0:T(8,128)} %winds.1, s32[32]{0:T(128)} %cutoff_in.1, f32[1,1536]{1,0:T(1,128)} %constant.6.clone.wave_in, ...), custom_call_target="tpu_custom_call" | custom-call | tf_op jit(solution)/shard_map/pallas_call | solution.py:679
  27.5 1.5 %shard_map.78 = (f32[2,4,32,1440]{3,2,1,0:T(8,128)}, f32[4,32,1440]{2,1,0:T(8,128)}) custom-call(f32[2,4,32,1440]{3,2,1,0:T(8,128)S(1)} %get-tuple-element.5.part_winds, f32[4,32,1440]{2,1,0:T(8,128)S(1)} %get-tuple-element.6.part_thick, f32[2,32,1440]{2,1,0:T(8,128)S(1)} %get-tuple-element.7.delta), custom_call_target="tpu_custom_call" | custom-call | tf_op jit(solution)/shard_map/pallas_call | solution.py:753

commit v6 on v5

--- a/solution.py
+++ b/solution.py
@@ -224,8 +224,8 @@
     x_up, x_down = ((x + 1) % chips) * 2 + core, ((x + chips - 1) % chips) * 2 + core
     has_minus, has_plus = lat > 0, lat < lat_count - 1
     lat_minus, lat_plus = jnp.maximum(lat - 1, 0), jnp.minimum(lat + 1, lat_count - 1)
-    early = (lat % 8 == 0) & (lat > 0)
-    after_early = lat % 8 == 1
+    follows = (lat % 8 == 0) & has_minus
+    leads = (lat % 8 == 7) & has_plus
 
     barrier = pltpu.get_barrier_semaphore()
     for device in ((lat, partner), (lat, x_up), (lat, x_down), (lat, chip_at(x + 2))):
@@ -235,7 +235,7 @@
     def _():
         pl.semaphore_signal(barrier, inc=1, device_id=(lat_minus, lev), device_id_type=MESH)
 
-    @pl.when(has_plus)
+    @pl.when(has_plus & jnp.logical_not(leads))
     def _():
         pl.semaphore_signal(barrier, inc=1, device_id=(lat_plus, lev), device_id_type=MESH)
 
@@ -355,8 +355,8 @@
     shares = [remote(column.at[*p], shared.at[*c], 3 + 2 * count + i, (lat, partner)) for i, (p, c) in enumerate(zip(places, pieces))]
 
     def enter():
-        pl.semaphore_wait(barrier, 4 + one(has_minus) + one(has_plus))
-        @pl.when(has_minus)
+        pl.semaphore_wait(barrier, 4 + one(has_minus & jnp.logical_not(follows)) + one(has_plus))
+        @pl.when(has_minus & jnp.logical_not(follows))
         def _():
             row_minus.start()
 
@@ -366,7 +366,7 @@
 
         to_pair.start()
 
-        @pl.when(has_minus)
+        @pl.when(has_minus & jnp.logical_not(follows))
         def _():
             to_minus.start()
 
@@ -429,8 +429,12 @@
     def rows_in():
         @pl.when(has_minus)
         def _():
-            row_minus.wait_send()
             row_plus.wait_recv()
+
+        @pl.when(follows)
+        def _():
+            row_minus.start()
+            to_minus.start()
 
         @pl.when(jnp.logical_not(has_minus))
         def _():
@@ -450,6 +454,7 @@
     def neighbours():
         @pl.when(has_minus)
         def _():
+            row_minus.wait_send()
             to_minus.wait_send()
             to_plus.wait_recv()
 
@@ -558,20 +563,15 @@
 
     some = lambda stage, *args: functools.partial(stage, *args)
 
-    @pl.when(early)
-    def _():
-        run(rest_of_loads, limits, forward_thick, forward_winds, some(products, range(6)), inverse)
-        run(some(inside, 0, RADIX), write_first, write_middle)
-        run(enter, first_step, rows_in, some(second_step, range(count // 2)), row_first)
-        run(some(second_step, range(count // 2, count)), share, neighbours)
-
-    @pl.when(after_early)
+    turn = follows | leads
+
+    @pl.when(turn)
     def _():
         run(enter, limits, forward_thick, first_step, rest_of_loads, forward_winds, some(products, range(3)))
         run(some(second_step, range(count)), some(products, range(3, 6)), share, inverse, some(inside, 0, RADIX))
-        run(write_first, rows_in, write_middle, row_first, neighbours)
-
-    @pl.when(jnp.logical_not(early | after_early))
+        run(write_first, write_middle, rows_in, row_first, neighbours)
+
+    @pl.when(jnp.logical_not(turn))
     def _():
         run(enter, limits, forward_thick, first_step, rest_of_loads, forward_winds, some(products, range(3)))
         run(some(second_step, range(count)), rows_in, some(products, range(3, 6)), row_first, inverse, share)

time: 29.2 us -> 27 us (0.925)
  the two profiles are of different devices: /device:TPU:11 before, /device:TPU:48 now
where the time goes in v6:
time: 27 us; the launch traced here: 26.8 us
  Pallas kernels  26.2 us (97%)
  between operations  0.64 us (2%)
    pallas_call x1, Pallas kernels, step(): pl.pallas_call(functools.partial(step_kernel, shape['lat'], shape['lev'])...  24.7 us
    pallas_call x1, Pallas kernels, last(): pl.pallas_call(last_kernel, out_shape=(jax.ShapeDtypeStruct(part_winds.sh...  1.47 us

profile of v6, /device:TPU:48, one launch (start us, length us, event | category | flops | bytes accessed | tf_op | source)
XLA Modules:
  0.0 26.8 jit_solution(9472276310761777477)
XLA Ops:
  0.6 24.7 %shard_map.77 = (f32[2,4,32,1440]{3,2,1,0:T(8,128)S(1)}, f32[4,32,1440]{2,1,0:T(8,128)S(1)}, f32[2,32,1440]{2,1,0:T(8,128)S(1)}) custom-call(f32[4,32,1440]{2,1,0:T(8,128)} %thick.1, f32[2,4,32,1440]{3,2,1,0:T(8,128)} %winds.1, s32[32]{0:T(128)} %cutoff_in.1, f32[1,1536]{1,0:T(1,128)} %constant.6.clone.wave_in, ...), custom_call_target="tpu_custom_call" | custom-call | tf_op jit(solution)/shard_map/pallas_call | solution.py:679
  25.3 1.5 %shard_map.78 = (f32[2,4,32,1440]{3,2,1,0:T(8,128)}, f32[4,32,1440]{2,1,0:T(8,128)}) custom-call(f32[2,4,32,1440]{3,2,1,0:T(8,128)S(1)} %get-tuple-element.5.part_winds, f32[4,32,1440]{2,1,0:T(8,128)S(1)} %get-tuple-element.6.part_thick, f32[2,32,1440]{2,1,0:T(8,128)S(1)} %get-tuple-element.7.delta), custom_call_target="tpu_custom_call" | custom-call | tf_op jit(solution)/shard_map/pallas_call | solution.py:753

commit v7 on v6

--- a/solution.py
+++ b/solution.py
@@ -563,15 +563,24 @@
 
     some = lambda stage, *args: functools.partial(stage, *args)
 
-    turn = follows | leads
+    turn = follows | leads | (lat == 1)
+    wait_first = (lat == 0) & (lev > 0)
+
+    @pl.when(wait_first)
+    def _():
+        run(rest_of_loads, limits, forward_thick, forward_winds, some(products, range(6)))
+        run(enter, first_step, rows_in, some(second_step, range(count // 2)), row_first)
+        run(some(second_step, range(count // 2, count)), inverse, share)
+        run(some(inside, 0, RADIX), write_first, write_middle, neighbours)
 
     @pl.when(turn)
     def _():
         run(enter, limits, forward_thick, first_step, rest_of_loads, forward_winds, some(products, range(3)))
-        run(some(second_step, range(count)), some(products, range(3, 6)), share, inverse, some(inside, 0, RADIX))
-        run(write_first, write_middle, rows_in, row_first, neighbours)
-
-    @pl.when(jnp.logical_not(turn))
+        run(some(second_step, range(count)), some(products, range(3, 6)), share, inverse)
+        run(some(inside, 0, RADIX // 2), rows_in, some(inside, RADIX // 2, RADIX), row_first)
+        run(write_first, write_middle, neighbours)
+
+    @pl.when(jnp.logical_not(turn | wait_first))
     def _():
         run(enter, limits, forward_thick, first_step, rest_of_loads, forward_winds, some(products, range(3)))
         run(some(second_step, range(count)), rows_in, some(products, range(3, 6)), row_first, inverse, share)

time: 27 us -> 28.2 us (1.044)
  the two profiles are of different devices: /device:TPU:48 before, /device:TPU:3 now
where the time goes in v7:
time: 28.2 us; the launch traced here: 28 us
  Pallas kernels  27.4 us (97%)
  between operations  0.64 us (2%)
    pallas_call x1, Pallas kernels, step(): pl.pallas_call(functools.partial(step_kernel, shape['lat'], shape['lev'])...  25.9 us
    pallas_call x1, Pallas kernels, last(): pl.pallas_call(last_kernel, out_shape=(jax.ShapeDtypeStruct(part_winds.sh...  1.47 us

profile of v7, /device:TPU:3, one launch (start us, length us, event | category | flops | bytes accessed | tf_op | source)
XLA Modules:
  0.0 28.0 jit_solution(16795275467514312671)
XLA Ops:
  0.6 25.9 %shard_map.77 = (f32[2,4,32,1440]{3,2,1,0:T(8,128)S(1)}, f32[4,32,1440]{2,1,0:T(8,128)S(1)}, f32[2,32,1440]{2,1,0:T(8,128)S(1)}) custom-call(f32[4,32,1440]{2,1,0:T(8,128)} %thick.1, f32[2,4,32,1440]{3,2,1,0:T(8,128)} %winds.1, s32[32]{0:T(128)} %cutoff_in.1, f32[1,1536]{1,0:T(1,128)} %constant.6.clone.wave_in, ...), custom_call_target="tpu_custom_call" | custom-call | tf_op jit(solution)/shard_map/pallas_call | solution.py:688
  26.6 1.5 %shard_map.78 = (f32[2,4,32,1440]{3,2,1,0:T(8,128)}, f32[4,32,1440]{2,1,0:T(8,128)}) custom-call(f32[2,4,32,1440]{3,2,1,0:T(8,128)S(1)} %get-tuple-element.5.part_winds, f32[4,32,1440]{2,1,0:T(8,128)S(1)} %get-tuple-element.6.part_thick, f32[2,32,1440]{2,1,0:T(8,128)S(1)} %get-tuple-element.7.delta), custom_call_target="tpu_custom_call" | custom-call | tf_op jit(solution)/shard_map/pallas_call | solution.py:762

commit v8 on v6

--- a/solution.py
+++ b/solution.py
@@ -563,13 +563,13 @@
 
     some = lambda stage, *args: functools.partial(stage, *args)
 
-    turn = follows | leads
-
+    turn = follows | leads | (lat == 1)
     @pl.when(turn)
     def _():
         run(enter, limits, forward_thick, first_step, rest_of_loads, forward_winds, some(products, range(3)))
-        run(some(second_step, range(count)), some(products, range(3, 6)), share, inverse, some(inside, 0, RADIX))
-        run(write_first, write_middle, rows_in, row_first, neighbours)
+        run(some(second_step, range(count)), some(products, range(3, 6)), share, inverse)
+        run(some(inside, 0, RADIX // 2), rows_in, some(inside, RADIX // 2, RADIX), row_first)
+        run(write_first, write_middle, neighbours)
 
     @pl.when(jnp.logical_not(turn))
     def _():

time: 27 us -> 26.3 us (0.974)
  the two profiles are of different devices: /device:TPU:48 before, /device:TPU:1 now
where the time goes in v8:
time: 26.3 us; the launch traced here: 26.2 us
  Pallas kernels  25.5 us (97%)
  between operations  0.64 us (2%)
    pallas_call x1, Pallas kernels, step(): pl.pallas_call(functools.partial(step_kernel, shape['lat'], shape['lev'])...  24.1 us
    pallas_call x1, Pallas kernels, last(): pl.pallas_call(last_kernel, out_shape=(jax.ShapeDtypeStruct(part_winds.sh...  1.47 us

profile of v8, /device:TPU:1, one launch (start us, length us, event | category | flops | bytes accessed | tf_op | source)
XLA Modules:
  0.0 26.2 jit_solution(10596686102147921740)
XLA Ops:
  0.6 24.1 %shard_map.77 = (f32[2,4,32,1440]{3,2,1,0:T(8,128)S(1)}, f32[4,32,1440]{2,1,0:T(8,128)S(1)}, f32[2,32,1440]{2,1,0:T(8,128)S(1)}) custom-call(f32[4,32,1440]{2,1,0:T(8,128)} %thick.1, f32[2,4,32,1440]{3,2,1,0:T(8,128)} %winds.1, s32[32]{0:T(128)} %cutoff_in.1, f32[1,1536]{1,0:T(1,128)} %constant.6.clone.wave_in, ...), custom_call_target="tpu_custom_call" | custom-call | tf_op jit(solution)/shard_map/pallas_call | solution.py:679
  24.7 1.5 %shard_map.78 = (f32[2,4,32,1440]{3,2,1,0:T(8,128)}, f32[4,32,1440]{2,1,0:T(8,128)}) custom-call(f32[2,4,32,1440]{3,2,1,0:T(8,128)S(1)} %get-tuple-element.5.part_winds, f32[4,32,1440]{2,1,0:T(8,128)S(1)} %get-tuple-element.6.part_thick, f32[2,32,1440]{2,1,0:T(8,128)S(1)} %get-tuple-element.7.delta), custom_call_target="tpu_custom_call" | custom-call | tf_op jit(solution)/shard_map/pallas_call | solution.py:753
